TPU v7x, 32 devices: a whole 2x2x4 slice. The times are simulated.
32 devices in a mesh: rows: 8 (over z, x), chan: 4 (over y, core).
Axes of the slice: x: 2, y: 2, z: 4, core: 2. Of those that a mesh axis runs over, the one named last changes fastest.
Arguments:
- frames: bfloat16 [9, 32, 480, 256], P(None, 'rows', 'chan'), may hold values from -450 to 450
- spatial_weight: bfloat16 [256, 2304], P('rows'), may hold values from -0.125 to 0.125
- temporal_weight: bfloat16 [256, 768], P('rows'), may hold values from -0.21875 to 0.21875
- down_weight: bfloat16 [256, 2304], P('rows'), may hold values from -0.125 to 0.125
- norm_gain: float32 [256], replicated, may hold values from 0.5 to 1.5
- norm_shift: float32 [256], replicated, may hold values from -3 to 3
- down_bias: float32 [256], replicated, may hold values from -3 to 3
Outputs:
- latent: bfloat16 [9, 16, 240, 256], P(None, 'rows', 'chan')
All inputs are finite; a program needn't handle non-finite values.
Results may differ from a plain program's by a relative error of at most 0.0053.
Values may be sent and summed in bfloat16 or wider, within the bound.
No kernel may reach another device: no remote copies, remote signals or barrier semaphores. Data moves between devices by JAX's collectives and lax.ppermute only.
A program may use at most 128 MiB of HBM per device.

v0:
```python
import jax
import jax.numpy as jnp
from jax import lax
from jax.sharding import PartitionSpec as P

GROUPS = 32


epsilon = 1e-06


def extended_2(cells, sides, width):
    for axis, dim in sides:
        count = lax.axis_size(axis)
        ends = count - 1
        head = lax.slice_in_dim(cells, 0, width, axis=dim)
        tail = lax.slice_in_dim(cells, cells.shape[dim] - width, cells.shape[dim], axis=dim)
        cells = jnp.concatenate(
            [
                lax.ppermute(tail, axis, [(i, (i + 1) % count) for i in range(ends)]),
                cells,
                lax.ppermute(head, axis, [((i + 1) % count, i) for i in range(ends)]),
            ],
            axis=dim,
        )
    return cells


def passed_along(block, axis, distance):
    devices = range(lax.axis_size(axis))
    route = [(i - distance, i) for i in devices if i - distance in devices]
    return lax.ppermute(block, axis, route)


def spatial_taps(padded, weight_rows, width_out):
    rows_out = padded.shape[1] - 2
    cols_out = padded.shape[2] - 2
    summed = None
    for tap_index in range(9):
        row_offset = tap_index // 3
        col_offset = tap_index % 3
        window = padded[
            :, row_offset : row_offset + rows_out, col_offset : col_offset + cols_out, :
        ]
        weight_panel = weight_rows[:, tap_index * width_out : (tap_index + 1) * width_out]
        product = jnp.einsum(
            "fijc,co->fijo", window, weight_panel, preferred_element_type=jnp.float32
        )
        summed = product if summed is None else summed + product
    return summed


def temporal_taps(values, weight_rows, width_out):
    frame_count = values.shape[0]
    summed = None
    for tap_index in range(3):
        lag_frames = 2 - tap_index
        if lag_frames > 0:
            delayed = jnp.concatenate(
                [jnp.repeat(values[:1], lag_frames, axis=0), values[: frame_count - lag_frames]],
                axis=0,
            )
        else:
            delayed = values
        weight_panel = weight_rows[:, tap_index * width_out : (tap_index + 1) * width_out]
        product = jnp.einsum(
            "fijc,co->fijo", delayed, weight_panel, preferred_element_type=jnp.float32
        )
        summed = product if summed is None else summed + product
    return summed


def down_taps(extended, weight_rows, width_out):
    rows_out = (extended.shape[1] - 1) // 2
    cols_out = (extended.shape[2] - 1) // 2
    summed = None
    for tap_index in range(9):
        row_offset = tap_index // 3
        col_offset = tap_index % 3
        window = extended[
            :,
            row_offset : row_offset + 2 * rows_out : 2,
            col_offset : col_offset + 2 * cols_out : 2,
            :,
        ]
        weight_panel = weight_rows[:, tap_index * width_out : (tap_index + 1) * width_out]
        product = jnp.einsum(
            "fijc,co->fijo", window, weight_panel, preferred_element_type=jnp.float32
        )
        summed = product if summed is None else summed + product
    return summed


def group_reduce(partial_sums):
    return lax.psum(partial_sums, ("rows", "chan"))


def place_groups(channel_sums, group_width):
    local_sums = channel_sums.reshape(-1, group_width).sum(axis=1)
    return local_sums


def channel_values(group_vector, group_width):
    return jnp.repeat(group_vector, group_width)


def per_device(
    frames, spatial_weight, temporal_weight, down_weight, norm_gain, norm_shift, down_bias
):
    full_spatial, full_temporal, full_down = (
        lax.all_gather(spatial_weight, "rows", axis=0, tiled=True),
        lax.all_gather(temporal_weight, "rows", axis=0, tiled=True),
        lax.all_gather(down_weight, "rows", axis=0, tiled=True),
    )
    channels = full_spatial.shape[0]
    group_width = channels // GROUPS
    frame_count = frames.shape[0]
    rows_dev = frames.shape[1]
    width_all = frames.shape[2] * lax.axis_size("chan")
    cell_count = float(frame_count * rows_dev * lax.axis_size("rows") * width_all * group_width)
    padded = extended_2(frames, (("rows", 1), ("chan", 2)), 1)
    first = spatial_taps(padded, full_spatial, channels).astype(jnp.bfloat16)
    hidden = temporal_taps(first, full_temporal, channels)
    channel_sums = jnp.sum(hidden, axis=(0, 1, 2))
    totals = group_reduce(place_groups(channel_sums, group_width)[None])
    means = totals[0] / cell_count
    chan_mean = channel_values(means, group_width)
    centered = hidden - chan_mean
    spread = group_reduce(
        place_groups(jnp.sum(centered * centered, axis=(0, 1, 2)), group_width)[None]
    )
    variance = spread[0] / cell_count
    chan_var = channel_values(variance, group_width)
    act = jax.nn.silu(centered * lax.rsqrt(chan_var + epsilon) * norm_gain + norm_shift).astype(
        jnp.bfloat16
    )
    below = passed_along(act[:, :1], "rows", -1)
    extended = jnp.concatenate([act, below], axis=1)
    beside = passed_along(extended[:, :, :1], "chan", -1)
    extended = jnp.concatenate([extended, beside], axis=2)
    latent = down_taps(extended, full_down, channels) + down_bias
    return latent.astype(jnp.bfloat16)


def solution(mesh):
    placed = (
        P(None, "rows", "chan", None),
        P("rows", None),
        P("rows", None),
        P("rows", None),
        P(),
        P(),
        P(),
    )
    return jax.shard_map(
        per_device,
        mesh=mesh,
        in_specs=placed,
        out_specs=P(None, "rows", "chan", None),
        check_vma=False,
    )
```

profile of v0, /device:TPU:0, one launch (start us, length us, event | category | flops | bytes accessed | tf_op | source)
XLA Modules:
  0.0 318.5 jit_solution(4577024968184721207)
XLA Ops:
  9.4 5.7 %collective-permute-start = (bf16[9,1,120,256]{3,2,1,0:T(8,128)(2,1)S(1)}, bf16[9,1,120,256]{3,2,1,0:T(8,128)(2,1)}, u32[]{:S(2)}, u32[]{:S(2)}) collective-permute-start(bf16[9,1,120,256]{3,2,1,0:T(8,128)(2,1)S(1)} %get-tuple-element.9), channel_id=1, source_target_pairs={{0,4},{4,8},{8,12},{12,16},{16,20},{20,24},{24,28},{1,5},{5,9},{9,... | collective-permute-start | bytes 1658888 | tf_op jit(solution)/shard_map/ppermute | solution.py:20
  16.4 23.1 %collective-permute-done = bf16[9,1,120,256]{3,2,1,0:T(8,128)(2,1)} collective-permute-done((bf16[9,1,120,256]{3,2,1,0:T(8,128)(2,1)S(1)}, bf16[9,1,120,256]{3,2,1,0:T(8,128)(2,1)}, u32[]{:S(2)}, u32[]{:S(2)}) %collective-permute-start) | collective-permute-done | bytes 552992 | tf_op jit(solution)/shard_map/ppermute | solution.py:20
  44.8 33.7 %all_gather.10 = bf16[256,768]{1,0:T(8,128)(2,1)} all-gather(bf16[32,768]{1,0:T(8,128)(2,1)S(1)} %copy-done.12), channel_id=1, replica_groups=mesh['rows'=8,'chan'=4] {'rows'}, dimensions={0}, use_global_device_ids=true | all-gather | bytes 442368 | tf_op jit(solution)/shard_map/all_gather | solution.py:112
  79.8 3.8 %fusion.15 = f32[9,4,120,256]{3,2,1,0:T(8,128)} fusion(bf16[9,6,120,256]{3,2,1,0:T(8,128)(2,1)S(1)} %constant_dynamic-update-slice_fusion, bf16[9,6,1,256]{3,2,1,0:T(2,128)(2,1)S(1)} %collective-permute-done.2, bf16[256,2304]{1,0:T(8,128)(2,1)} %all-gather.3.cloned.1.call-done), kind=kOutput, calls=%fused_computation.29 | convolution fusion | flops 570654720 | bytes 7900160 | tf_op jit(solution)/shard_map/fijc,co->fijo/dot_general | solution.py:46
  83.6 2.9 fusion.18
  86.5 2.8 fusion.12
  89.3 2.9 fusion.9
  92.2 2.9 fusion.22
  95.1 3.9 %fusion = f32[9,4,120,256]{3,2,1,0:T(8,128)} fusion(bf16[9,4,120,256]{3,2,1,0:T(8,128)(2,1)S(1)} %copy-done, bf16[9,1,120,256]{3,2,1,0:T(8,128)(2,1)} %collective-permute-done, bf16[256,2304]{1,0:T(8,128)(2,1)S(1)} %copy-done.11), kind=kOutput, calls=%fused_computation.15 | convolution fusion | flops 571760640 | bytes 7319552 | tf_op jit(solution)/shard_map/fijc,co->fijo/dot_general | solution.py:46
  100.8 2.9 fusion.50
  103.7 12.6 %add_convert_fusion = bf16[9,4,120,256]{3,2,1,0:T(8,128)(2,1)} fusion(f32[9,4,120,256]{3,2,1,0:T(8,128)S(1)} %fusion.4, f32[9,4,120,256]{3,2,1,0:T(8,128)} %fusion.22, f32[9,4,120,256]{3,2,1,0:T(8,128)} %fusion.9, f32[9,4,120,256]{3,2,1,0:T(8,128)} %fusion.50, f32[9,4,120,256]{3,2,1,0:T(8,128)} %fusion.15, f32[9,4,120,256]{3,2,1,0:T(8,128)} %fusion.12, ...), kind=kOutput, calls=%fused_computation.7 | convolution fusion | flops 580608000 | bytes 41105408 | tf_op jit(solution)/shard_map/fijc,co->fijo/dot_general | solution.py:46
  121.9 3.0 fusion.65
  125.1 39.6 %psum.14 = f32[1,32]{1,0:T(1,128)S(1)} all-reduce(f32[1,32]{1,0:T(1,128)S(1)} %bitcast.127), channel_id=1, replica_groups=mesh['rows'=8,'chan'=4] {'rows','chan'}, use_global_device_ids=true, to_apply=%region_2.0 | all-reduce | flops 32 | bytes 256 | tf_op jit(solution)/shard_map/psum | solution.py:95
  164.9 2.9 multiply_reduce_fusion
  167.9 40.9 %psum.15 = f32[1,32]{1,0:T(1,128)S(1)} all-reduce(f32[1,32]{1,0:T(1,128)S(1)} %bitcast.126), channel_id=1, replica_groups=mesh['rows'=8,'chan'=4] {'rows','chan'}, use_global_device_ids=true, to_apply=%region_5.0 | all-reduce | flops 32 | bytes 256 | tf_op jit(solution)/shard_map/psum | solution.py:95
  209.1 3.6 %multiply_convert_fusion = bf16[9,4,120,256]{3,2,1,0:T(8,128)(2,1)S(1)} fusion(f32[9,4,120,256]{3,2,1,0:T(8,128)} %get-tuple-element.12, f32[256]{0:T(256)S(1)} %copy-done.13, f32[256]{0:T(256)S(1)} %copy-done.14, f32[256]{0:T(256)S(1)} %rsqrt.16, f32[256]{0:T(256)S(1)} %sub.10), kind=kLoop, calls=%fused_computation.4 | loop fusion | flops 9953280 | bytes 6639616 | tf_op jit(solution)/shard_map/convert_element_type | solution.py:134
  218.0 11.6 %collective-permute-done.4 = bf16[9,1,120,256]{3,2,1,0:T(8,128)(2,1)S(1)} collective-permute-done((bf16[9,1,120,256]{3,2,1,0:T(8,128)(2,1)}, bf16[9,1,120,256]{3,2,1,0:T(8,128)(2,1)S(1)}, u32[]{:S(2)}, u32[]{:S(2)}) %collective-permute-start.4) | collective-permute-done | bytes 552992 | tf_op jit(solution)/shard_map/ppermute | solution.py:32
  231.4 10.3 %slice.188 = bf16[9,2,60,256]{3,2,1,0:T(8,128)(2,1)} slice(bf16[9,5,120,256]{3,2,1,0:T(8,128)(2,1)} %pad_maximum_fusion), slice={[0:9:1], [1:5:2], [0:120:2], [0:256:1]} | slice | bytes 1105920 | tf_op jit(solution)/shard_map/slice | solution.py:80
  241.7 8.5 %slice.194 = bf16[9,2,60,256]{3,2,1,0:T(8,128)(2,1)S(1)} slice(bf16[9,5,120,256]{3,2,1,0:T(8,128)(2,1)} %pad_maximum_fusion), slice={[0:9:1], [2:5:2], [0:120:2], [0:256:1]} | slice | bytes 1105920 | tf_op jit(solution)/shard_map/slice | solution.py:80
  258.2 10.5 %slice.184 = bf16[9,2,60,256]{3,2,1,0:T(8,128)(2,1)} slice(bf16[9,5,121,256]{3,2,1,0:T(8,128)(2,1)} %pad_maximum_fusion.1), slice={[0:9:1], [0:4:2], [1:121:2], [0:256:1]} | slice | bytes 1105920 | tf_op jit(solution)/shard_map/slice | solution.py:80
  268.6 10.2 %slice.198 = bf16[9,2,60,256]{3,2,1,0:T(8,128)(2,1)} slice(bf16[9,5,121,256]{3,2,1,0:T(8,128)(2,1)} %pad_maximum_fusion.1), slice={[0:9:1], [2:5:2], [2:121:2], [0:256:1]} | slice | bytes 1105920 | tf_op jit(solution)/shard_map/slice | solution.py:80
  278.8 10.1 %slice.196 = bf16[9,2,60,256]{3,2,1,0:T(8,128)(2,1)} slice(bf16[9,5,121,256]{3,2,1,0:T(8,128)(2,1)} %pad_maximum_fusion.1), slice={[0:9:1], [2:5:2], [1:121:2], [0:256:1]} | slice | bytes 1105920 | tf_op jit(solution)/shard_map/slice | solution.py:80
  288.9 6.0 %slice.192 = bf16[9,2,60,256]{3,2,1,0:T(8,128)(2,1)} slice(bf16[9,5,121,256]{3,2,1,0:T(8,128)(2,1)S(1)} %copy-done.2), slice={[0:9:1], [1:5:2], [2:121:2], [0:256:1]} | slice | bytes 1105920 | tf_op jit(solution)/shard_map/slice | solution.py:80
  294.9 5.9 %slice.190 = bf16[9,2,60,256]{3,2,1,0:T(8,128)(2,1)} slice(bf16[9,5,121,256]{3,2,1,0:T(8,128)(2,1)S(1)} %copy-done.2), slice={[0:9:1], [1:5:2], [1:121:2], [0:256:1]} | slice | bytes 1105920 | tf_op jit(solution)/shard_map/slice | solution.py:80
  (87 shorter events, 44.7 us)
Async XLA Ops:
  6.5 73.3 %all-gather.3.cloned.1.call-start = ((), (), s32[]{:S(2)}) async-start(), calls=%async_computation | async-start | bytes 1327104 | tf_op jit(solution)/shard_map/all_gather | solution.py:111
  7.3 208.5 %all-gather.5.cloned.1.call-start = ((), (), s32[]{:S(2)}) async-start(), calls=%async_computation.1 | async-start | bytes 1327104 | tf_op jit(solution)/shard_map/all_gather | solution.py:113
  9.4 30.0 %collective-permute-start = (bf16[9,1,120,256]{3,2,1,0:T(8,128)(2,1)S(1)}, bf16[9,1,120,256]{3,2,1,0:T(8,128)(2,1)}, u32[]{:S(2)}, u32[]{:S(2)}) collective-permute-start(bf16[9,1,120,256]{3,2,1,0:T(8,128)(2,1)S(1)} %get-tuple-element.9), channel_id=1, source_target_pairs={{0,4},{4,8},{8,12},{12,16},{16,20},{20,24},{24,28},{1,5},{5,9},{9,... | collective-permute-start | bytes 1658888 | tf_op jit(solution)/shard_map/ppermute | solution.py:20
  15.1 27.3 %collective-permute-start.1 = (bf16[9,1,120,256]{3,2,1,0:T(8,128)(2,1)}, bf16[9,1,120,256]{3,2,1,0:T(8,128)(2,1)}, u32[]{:S(2)}, u32[]{:S(2)}) collective-permute-start(bf16[9,1,120,256]{3,2,1,0:T(8,128)(2,1)} %get-tuple-element.10), channel_id=1, source_target_pairs={{4,0},{8,4},{12,8},{16,12},{20,16},{24,20},{28,24},{5,1},{9,5},{13... | collective-permute-start | bytes 1658888 | tf_op jit(solution)/shard_map/ppermute | solution.py:22
  40.5 4.3 %copy-start.12 = (bf16[32,768]{1,0:T(8,128)(2,1)S(1)}, bf16[32,768]{1,0:T(8,128)(2,1)}, u32[]{:S(2)}) copy-start(bf16[32,768]{1,0:T(8,128)(2,1)} %param.9) | copy-start | bytes 147460
  43.5 36.3 %collective-permute-start.2 = (bf16[9,6,1,256]{3,2,1,0:T(2,128)(2,1)S(1)}, bf16[9,6,1,256]{3,2,1,0:T(2,128)(2,1)S(1)}, u32[]{:S(2)}, u32[]{:S(2)}) collective-permute-start(bf16[9,6,1,256]{3,2,1,0:T(2,128)(2,1)S(1)} %get-tuple-element.6), channel_id=1, source_target_pairs={{0,1},{1,2},{2,3},{4,5},{5,6},{6,7},{8,9},{9,10},{10,11},{12,13},{... | collective-permute-start | bytes 82952 | tf_op jit(solution)/shard_map/ppermute | solution.py:20
  78.5 8.0 %collective-permute-start.3 = (bf16[9,6,1,256]{3,2,1,0:T(2,128)(2,1)S(1)}, bf16[9,6,1,256]{3,2,1,0:T(2,128)(2,1)S(1)}, u32[]{:S(2)}, u32[]{:S(2)}) collective-permute-start(bf16[9,6,1,256]{3,2,1,0:T(2,128)(2,1)S(1)} %get-tuple-element.5), channel_id=1, source_target_pairs={{1,0},{2,1},{3,2},{5,4},{6,5},{7,6},{9,8},{10,9},{11,10},{13,12},{... | collective-permute-start | bytes 82952 | tf_op jit(solution)/shard_map/ppermute | solution.py:22
  79.8 3.8 %copy-start.11 = (bf16[256,2304]{1,0:T(8,128)(2,1)S(1)}, bf16[256,2304]{1,0:T(8,128)(2,1)}, u32[]{:S(2)}) copy-start(bf16[256,2304]{1,0:T(8,128)(2,1)} %all-gather.3.cloned.1.call-done) | copy-start | bytes 3538948
  92.2 2.9 copy-start
  116.3 1.6 copy-start.1
  120.4 1.5 slice-start.1
  124.9 84.1 %copy-start.13 = (f32[256]{0:T(256)S(1)}, f32[256]{0:T(256)}, u32[]{:S(2)}) copy-start(f32[256]{0:T(256)} %param.12) | copy-start | bytes 3076
  124.9 84.1 %copy-start.14 = (f32[256]{0:T(256)S(1)}, f32[256]{0:T(256)}, u32[]{:S(2)}) copy-start(f32[256]{0:T(256)} %param.11) | copy-start | bytes 3076
  213.5 16.1 %collective-permute-start.4 = (bf16[9,1,120,256]{3,2,1,0:T(8,128)(2,1)}, bf16[9,1,120,256]{3,2,1,0:T(8,128)(2,1)S(1)}, u32[]{:S(2)}, u32[]{:S(2)}) collective-permute-start(bf16[9,1,120,256]{3,2,1,0:T(8,128)(2,1)} %slice.226), channel_id=1, source_target_pairs={{4,0},{8,4},{12,8},{16,12},{20,16},{24,20},{28,24},{5,1},{9,5},{13... | collective-permute-start | bytes 1658888 | tf_op jit(solution)/shard_map/ppermute | solution.py:32
  250.2 1.5 copy-start.8
  250.3 5.9 %collective-permute-start.5 = (bf16[9,5,1,256]{3,2,1,0:T(2,128)(2,1)S(1)}, bf16[9,5,1,256]{3,2,1,0:T(2,128)(2,1)S(1)}, u32[]{:S(2)}, u32[]{:S(2)}) collective-permute-start(bf16[9,5,1,256]{3,2,1,0:T(2,128)(2,1)S(1)} %fusion.51), channel_id=1, source_target_pairs={{1,0},{2,1},{3,2},{5,4},{6,5},{7,6},{9,8},{10,9},{11,10},{13,12},{... | collective-permute-start | bytes 69128 | tf_op jit(solution)/shard_map/ppermute | solution.py:32
  258.2 30.7 %copy-start.2 = (bf16[9,5,121,256]{3,2,1,0:T(8,128)(2,1)S(1)}, bf16[9,5,121,256]{3,2,1,0:T(8,128)(2,1)}, u32[]{:S(2)}) copy-start(bf16[9,5,121,256]{3,2,1,0:T(8,128)(2,1)} %pad_maximum_fusion.1) | copy-start | bytes 8363524
  301.8 3.1 copy-start.9
  301.8 4.3 %copy-start.7 = (bf16[9,2,60,256]{3,2,1,0:T(8,128)(2,1)S(1)}, bf16[9,2,60,256]{3,2,1,0:T(8,128)(2,1)}, u32[]{:S(2)}) copy-start(bf16[9,2,60,256]{3,2,1,0:T(8,128)(2,1)} %slice.190) | copy-start | bytes 1658884
  303.3 4.2 %copy-start.5 = (f32[9,2,60,256]{3,2,1,0:T(8,128)S(1)}, f32[9,2,60,256]{3,2,1,0:T(8,128)}, u32[]{:S(2)}) copy-start(f32[9,2,60,256]{3,2,1,0:T(8,128)} %fusion.48) | copy-start | bytes 3317764
  303.4 4.2 %copy-start.6 = (bf16[9,2,60,256]{3,2,1,0:T(8,128)(2,1)S(1)}, bf16[9,2,60,256]{3,2,1,0:T(8,128)(2,1)}, u32[]{:S(2)}) copy-start(bf16[9,2,60,256]{3,2,1,0:T(8,128)(2,1)} %slice.184) | copy-start | bytes 1658884
  306.1 2.6 copy-start.3
  306.1 2.6 copy-start.4
  306.1 2.6 copy-start.15
  (2 other events, 2.5 us)
Sparse Core Ops, SparseCore 0:
  9.5 55.3 all-gather.2
  67.1 40.4 all-gather.4
where the time goes:
time: 322 us; the launch traced here: 319 us
  blocking collectives  114 us (35%)
  local copies, waits for them, and re-layouts  76.4 us (24%)
  matrix products  56 us (17%)
  waiting for transfers between devices  35.5 us (11%)
  between operations  13.8 us (4%)
  starting transfers between devices  12.3 us (4%)
  other arithmetic  10.5 us (3%)
    psum x2, blocking collectives, group_reduce(): return lax.psum(partial_sums, ('rows', 'chan'))  80.5 us
    slice x9, local copies, waits for them, and re-layouts, down_taps(): extended[:, row_offset:row_offset + 2 * rows_out:2, col_offset:col_offset...  63.3 us
    dot_general x9, matrix products, spatial_taps(): jnp.einsum('fijc,co->fijo', window, weight_panel, preferred_element_type=...  36.4 us
    all_gather x1, blocking collectives, per_device(): lax.all_gather(temporal_weight, 'rows', axis=0, tiled=True)  33.7 us
    ppermute x2, waiting for transfers between devices, extended_2(): lax.ppermute(tail, axis, [(i, (i + 1) % count) for i in range(ends)])  23.1 us
    dot_general x9, matrix products, down_taps(): jnp.einsum('fijc,co->fijo', window, weight_panel, preferred_element_type=...  15.1 us
    ppermute x2, waiting for transfers between devices, passed_along(): return lax.ppermute(block, axis, route)  11.6 us
    ppermute x2, starting transfers between devices, extended_2(): lax.ppermute(tail, axis, [(i, (i + 1) % count) for i in range(ends)])  6.96 us
  transfers between devices with their start and end apart: 8, of which 2 were waited for; matrix products, arithmetic and copies ran while one was open for 20% of the time, Pallas kernels for 0%

commit v1 on v0

v1 whole, which is shorter than its diff:
```python
import functools

import jax
import jax.numpy as jnp
from jax import lax
from jax.experimental import pallas as pl
from jax.experimental.pallas import tpu as pltpu
from jax.sharding import PartitionSpec as P

GROUPS = 32
EPSILON = 1e-06
LANE_COLS = 128
F32 = jnp.float32
BF16 = jnp.bfloat16


def shifted(block, axis, distance):
    count = lax.axis_size(axis)
    route = [(i, i + distance) for i in range(count) if 0 <= i + distance < count]
    return lax.ppermute(block, axis, route)


def swapped(block, axis, bit):
    return lax.ppermute(block, axis, [(i, i ^ bit) for i in range(lax.axis_size(axis))])


def weight_parts(weight):
    chan = lax.axis_size("chan")
    part = weight.shape[0] // chan
    own = lax.dynamic_slice_in_dim(weight, lax.axis_index("chan") * part, part, 0)
    return own


def spread_rows(own):
    rows = lax.axis_size("rows")
    return lax.all_to_all(jnp.broadcast_to(own[None], (rows,) + own.shape), "rows", 0, 0)


def spread_chan(held):
    parts = [held]
    bit = lax.axis_size("chan") // 2
    while bit:
        parts = parts + [swapped(part, "chan", bit) for part in parts]
        bit //= 2
    order = [0]
    bit = lax.axis_size("chan") // 2
    while bit:
        order = order + [o ^ bit for o in order]
        bit //= 2
    return [parts[order.index(k)] for k in range(len(order))]


def assemble(chan_index, parts, wide, weight):
    for k, part in enumerate(parts):
        wide[:, chan_index ^ k] = part[...].astype(F32)
    weight[...] = wide[...].reshape(weight.shape).astype(BF16)


def front_kernel(
    index, frames, top, bottom, pack, pack_top, pack_bottom, *rest, parts, channels, n_frames
):
    part_refs = rest[:parts]
    first_row, hidden, stats, temporal, wide, weight, x, held, moments = rest[parts:]
    step = pl.program_id(0)
    rows, cols = frames.shape[1], frames.shape[2]

    @pl.when(step == 0)
    def _():
        assemble(index[1], part_refs, wide, weight)
        temporal[...] = weight[:, 9 * channels :]

    def joined(main, side):
        return jnp.concatenate([main.astype(F32), side.astype(F32)], axis=1).astype(BF16)

    x[0] = joined(top[0], pack_top[0])[0]
    x[1 : rows + 1] = joined(frames[0], pack[0])
    x[rows + 1] = joined(bottom[0], pack_bottom[0])[0]
    size = rows * LANE_COLS
    products = []
    for b in range(3):
        total = None
        for a in range(3):
            tap = 3 * a + b
            lhs = x[a : a + rows].reshape(size, channels)
            term = jnp.dot(
                lhs,
                weight[:, tap * channels : (tap + 1) * channels],
                preferred_element_type=F32,
            )
            total = term if total is None else total + term
        products.append(total.reshape(rows, LANE_COLS, channels))
    first = (
        products[1]
        + pltpu.roll(products[0], 1, 1)
        + pltpu.roll(products[2], LANE_COLS - 1, 1)
    )
    first = first.astype(BF16)
    first_row[0] = first[0]
    first = first.reshape(size, channels)

    @pl.when(step == 0)
    def _():
        held[0] = first
        held[1] = first

    slot = lax.rem(step, 2)
    base = 9 * channels
    total = (
        jnp.dot(held[slot], weight[:, base : base + channels], preferred_element_type=F32)
        + jnp.dot(
            held[1 - slot],
            weight[:, base + channels : base + 2 * channels],
            preferred_element_type=F32,
        )
        + jnp.dot(first, weight[:, base + 2 * channels :], preferred_element_type=F32)
    )
    held[slot] = first
    total = total.reshape(rows, LANE_COLS, channels)
    for k in range(channels // 128):
        hidden[0, :, k] = total[:, :, k * 128 : (k + 1) * 128]
    inner = total[:, :cols].reshape(rows * cols, channels)
    count = float(rows * cols)
    mean = jnp.sum(inner, axis=0, keepdims=True) / count
    spread = jnp.sum(jnp.square(inner - mean), axis=0, keepdims=True)

    @pl.when(step == 0)
    def _():
        moments[0:1] = mean
        moments[1:2] = spread

    @pl.when(step > 0)
    def _():
        done = step.astype(F32)
        delta = mean - moments[0:1]
        moments[0:1] = moments[0:1] + delta / (done + 1.0)
        moments[1:2] = moments[1:2] + spread + delta * delta * (count * done / (done + 1.0))

    @pl.when(step == n_frames - 1)
    def _():
        stats[...] = jnp.broadcast_to(moments[0:2][None], stats.shape)


def back_kernel(
    index, hidden, halo, temporal, stats, gain, shift, bias, *rest, parts, channels, count
):
    part_refs = rest[:parts]
    latent, wide, weight, affine, full, even, odd = rest[parts:]
    step = pl.program_id(0)
    batch, rows = hidden.shape[0], hidden.shape[1]
    half = LANE_COLS // 2
    cols_out = latent.shape[2]
    rows_out = rows // 2
    blocks = channels // 128

    @pl.when(step == 0)
    def _():
        assemble(index[1], part_refs, wide, weight)
        devices = stats.shape[0]
        group = channels // GROUPS
        means = stats[:, 0]
        mean = jnp.sum(means, axis=0, keepdims=True) / float(devices)
        spread = jnp.sum(stats[:, 1], axis=0, keepdims=True) + count * jnp.sum(
            jnp.square(means - mean), axis=0, keepdims=True
        )
        lane = lax.broadcasted_iota(jnp.int32, (channels, channels), 0) // group
        same = lane == lax.broadcasted_iota(jnp.int32, (channels, channels), 1) // group
        same = same.astype(F32)

        def over_group(values):
            return jnp.dot(
                jnp.broadcast_to(values, (8, channels)),
                same,
                precision=lax.Precision.HIGHEST,
                preferred_element_type=F32,
            )[0:1] / float(group)

        group_mean = over_group(mean)
        total = over_group(spread / (count * devices) + jnp.square(mean - group_mean))
        affine[0:1] = group_mean
        affine[1:2] = lax.rsqrt(total + EPSILON)

    mean = affine[0:1]
    rstd = affine[1:2]
    for i in range(batch):
        frame = step * batch + i
        older = jnp.maximum(frame - 2, 0)
        old = jnp.maximum(frame - 1, 0)
        extra = (
            jnp.dot(halo[older], temporal[:, :channels], preferred_element_type=F32)
            + jnp.dot(
                halo[old], temporal[:, channels : 2 * channels], preferred_element_type=F32
            )
            + jnp.dot(halo[frame], temporal[:, 2 * channels :], preferred_element_type=F32)
        )
        for k in range(blocks):
            full[i, k] = extra[:, k * 128 : (k + 1) * 128]

    def columns(i, row, start):
        picked = pl.ds(start, half, stride=2)
        return jnp.concatenate(
            [
                hidden[i, row, k, picked] if row < rows else full[i, k, picked]
                for k in range(blocks)
            ],
            axis=1,
        )

    def activated(values):
        return jax.nn.silu((values - mean) * rstd * gain[...] + shift[...])

    for i in range(batch):
        for row in range(rows + 1):
            place = row // 2 if row % 2 == 0 else rows_out + 1 + row // 2
            e = activated(columns(i, row, 0))
            o = activated(columns(i, row, 1))
            at = lax.broadcasted_iota(jnp.int32, e.shape, 0)
            keep = (index[3] == 0) | (at < cols_out)
            if row == rows:
                keep = keep & (index[2] == 0)
                o = jnp.where(index[2] == 0, o, 0.0)
            e = jnp.where(keep, e, 0.0)
            even[place, i] = e.astype(BF16)
            odd[place, i] = o.astype(BF16)
    size = rows_out * batch * half
    starts = (0, rows_out + 1, 1)
    sums = []
    for source, taps in ((even, (0,)), (odd, (1,)), (even, (2,))):
        total = None
        for a in range(3):
            lhs = source[starts[a] : starts[a] + rows_out].reshape(size, channels)
            tap = 3 * a + taps[0]
            term = jnp.dot(
                lhs,
                weight[:, tap * channels : (tap + 1) * channels],
                preferred_element_type=F32,
            )
            total = term if total is None else total + term
        sums.append(total.reshape(rows_out * batch, half, channels))
    out = sums[0] + sums[1] + pltpu.roll(sums[2], half - 1, 1) + bias[...]
    out = out.reshape(rows_out, batch, half, channels).astype(BF16)
    for p in range(rows_out):
        for i in range(batch):
            latent[i, p] = out[p, i, :cols_out]


def whole(shape):
    return pl.BlockSpec(shape, lambda i, *_: (0,) * len(shape))


def gathered_parts(weight):
    chan = lax.axis_size("chan")
    if weight.shape[0] % (8 * chan) == 0:
        own = weight_parts(weight)
        return own, True
    return lax.all_gather(weight, "rows", axis=0, tiled=True), False


def per_device(
    frames, spatial_weight, temporal_weight, down_weight, norm_gain, norm_shift, down_bias
):
    n_frames, rows, cols, channels = frames.shape
    row_devices, chan_devices = lax.axis_size("rows"), lax.axis_size("chan")
    row_index, chan_index = lax.axis_index("rows"), lax.axis_index("chan")
    index = jnp.stack(
        [
            row_index,
            chan_index,
            (row_index == row_devices - 1).astype(jnp.int32),
            (chan_index == chan_devices - 1).astype(jnp.int32),
        ]
    ).astype(jnp.int32)

    top = shifted(frames[:, rows - 1 :], "rows", 1)
    bottom = shifted(frames[:, :1], "rows", -1)
    right = shifted(frames[:, :, :8], "chan", -1)
    left = shifted(frames[:, :, cols - 8 :], "chan", 1)
    at = lax.broadcasted_iota(jnp.int32, right.shape, 2)
    pack = jnp.where(at == 7, left, right)
    pack_top = shifted(pack[:, rows - 1 :], "rows", 1)
    pack_bottom = shifted(pack[:, :1], "rows", -1)

    split = spatial_weight.shape[0] % (8 * chan_devices) == 0
    if split:
        own = jnp.concatenate([weight_parts(spatial_weight), weight_parts(temporal_weight)], 1)
        front_parts = spread_chan(spread_rows(own))
        back_parts = spread_chan(
            lax.all_gather(weight_parts(down_weight), "rows", axis=0, tiled=False)
        )
    else:
        joint = jnp.concatenate([spatial_weight, temporal_weight], 1)
        front_parts = [lax.all_gather(joint, "rows", axis=0, tiled=True)]
        back_parts = [lax.all_gather(down_weight, "rows", axis=0, tiled=True)]
        front_parts = [front_parts[0].reshape(channels // 8, 8, -1)]
        back_parts = [back_parts[0].reshape(channels // 8, 8, -1)]
        index = index.at[1].set(0)
    parts = len(front_parts)
    piece = front_parts[0].shape
    wide_front = (piece[0], parts, piece[1], piece[2])
    piece_back = back_parts[0].shape
    wide_back = (piece_back[0], parts, piece_back[1], piece_back[2])

    frame_block = lambda *tail: pl.BlockSpec((1,) + tail, lambda i, *_: (i,) + (0,) * len(tail))
    flops = 2 * n_frames * rows * LANE_COLS * channels * channels
    first_row, hidden, stats, temporal = pl.pallas_call(
        functools.partial(front_kernel, parts=parts, channels=channels, n_frames=n_frames),
        grid_spec=pltpu.PrefetchScalarGridSpec(
            num_scalar_prefetch=1,
            grid=(n_frames,),
            in_specs=[
                frame_block(rows, cols, channels),
                frame_block(1, cols, channels),
                frame_block(1, cols, channels),
                frame_block(rows, 8, channels),
                frame_block(1, 8, channels),
                frame_block(1, 8, channels),
            ]
            + [whole(piece)] * parts,
            out_specs=[
                frame_block(LANE_COLS, channels),
                frame_block(rows, channels // 128, LANE_COLS, 128),
                whole((row_devices * chan_devices, 2, channels)),
                whole((channels, 3 * channels)),
            ],
            scratch_shapes=[
                pltpu.VMEM(wide_front, F32),
                pltpu.VMEM((channels, 12 * channels), BF16),
                pltpu.VMEM((rows + 2, LANE_COLS, channels), BF16),
                pltpu.VMEM((2, rows * LANE_COLS, channels), BF16),
                pltpu.VMEM((8, channels), F32),
            ],
        ),
        out_shape=[
            jax.ShapeDtypeStruct((n_frames, LANE_COLS, channels), BF16),
            jax.ShapeDtypeStruct((n_frames, rows, channels // 128, LANE_COLS, 128), F32),
            jax.ShapeDtypeStruct((row_devices * chan_devices, 2, channels), F32),
            jax.ShapeDtypeStruct((channels, 3 * channels), BF16),
        ],
        compiler_params=pltpu.CompilerParams(
            dimension_semantics=("arbitrary",), vmem_limit_bytes=40 << 20
        ),
        cost_estimate=pl.CostEstimate(
            flops=12 * flops, bytes_accessed=12 << 20, transcendentals=0
        ),
        name="front",
    )(index, frames, top, bottom, pack, pack_top, pack_bottom, *front_parts)

    halo = shifted(first_row, "rows", -1)
    all_stats = lax.all_to_all(stats, ("rows", "chan"), 0, 0)

    batch = 3 if n_frames % 3 == 0 else 1
    vector = lambda v: v.reshape(1, channels)
    rows_out, cols_out = rows // 2, cols // 2
    batch_block = lambda *tail: pl.BlockSpec(
        (batch,) + tail, lambda i, *_: (i,) + (0,) * len(tail)
    )
    return pl.pallas_call(
        functools.partial(
            back_kernel, parts=parts, channels=channels, count=float(n_frames * rows * cols)
        ),
        grid_spec=pltpu.PrefetchScalarGridSpec(
            num_scalar_prefetch=1,
            grid=(n_frames // batch,),
            in_specs=[
                batch_block(rows, channels // 128, LANE_COLS, 128),
                whole((n_frames, LANE_COLS, channels)),
                whole((channels, 3 * channels)),
                whole(all_stats.shape),
                whole((1, channels)),
                whole((1, channels)),
                whole((1, channels)),
            ]
            + [whole(piece_back)] * parts,
            out_specs=batch_block(rows_out, cols_out, channels),
            scratch_shapes=[
                pltpu.VMEM(wide_back, F32),
                pltpu.VMEM((channels, 9 * channels), BF16),
                pltpu.VMEM((8, channels), F32),
                pltpu.VMEM((batch, channels // 128, LANE_COLS, 128), F32),
                pltpu.VMEM((rows + 1, batch, LANE_COLS // 2, channels), BF16),
                pltpu.VMEM((rows + 1, batch, LANE_COLS // 2, channels), BF16),
            ],
        ),
        out_shape=jax.ShapeDtypeStruct((n_frames, rows_out, cols_out, channels), BF16),
        compiler_params=pltpu.CompilerParams(
            dimension_semantics=("arbitrary",), vmem_limit_bytes=40 << 20
        ),
        cost_estimate=pl.CostEstimate(
            flops=3 * flops, bytes_accessed=10 << 20, transcendentals=4 << 20
        ),
        name="back",
    )(
        index,
        hidden,
        halo,
        temporal,
        all_stats,
        vector(norm_gain),
        vector(norm_shift),
        vector(down_bias),
        *back_parts,
    )


def solution(mesh):
    placed = (
        P(None, "rows", "chan", None),
        P("rows", None),
        P("rows", None),
        P("rows", None),
        P(),
        P(),
        P(),
    )
    return jax.shard_map(
        per_device,
        mesh=mesh,
        in_specs=placed,
        out_specs=P(None, "rows", "chan", None),
        check_vma=False,
    )
```

time: 322 us -> 124 us (0.39)
  blocking collectives: 114 us -> 32 us
  local copies, waits for them, and re-layouts: 76.4 us -> 14.1 us
  matrix products: 56 us -> 0 us
  Pallas kernels: 0 us -> 22.6 us
  starting transfers between devices: 12.3 us -> 33.6 us
  waiting for transfers between devices: 35.5 us -> 20.5 us
  between operations: 13.8 us -> 0.19 us
  other arithmetic: 10.5 us -> 0.18 us
    psum x2 -> x0, blocking collectives: 80.5 us -> none  [group_reduce(): return lax.psum(partial_sums, ('rows', 'chan'))]
    slice x17 -> x3, local copies, waits for them, and re-layouts: 67.9 us -> 3.29 us  [the longest x1 2.28 us: per_device(): bottom = shifted(frames[:, :1], 'rows', -1)]
    dot_general x21 -> x0, matrix products: 56 us -> none  [the longest x9 36.4 us: spatial_taps(): jnp.einsum('fijc,co->fijo', window, weight_panel, preferred_element_type=...]
    pallas_call x0 -> x2, Pallas kernels: none -> 22.6 us  [the longest x1 18.6 us: per_device(): pl.pallas_call(functools.partial(front_kernel, parts=parts, channels=chan...]
    ppermute x6 -> x13, waiting for transfers between devices: 34.7 us -> 12.8 us  [the longest x6 8.28 us: swapped(): lax.ppermute(block, axis, [(i, i ^ bit) for i in range(lax.axis_size(axis...]
    ppermute x6 -> x13, starting transfers between devices: 12.2 us -> 23.2 us  [the longest x7 15.5 us: shifted(): return lax.ppermute(block, axis, route)]
    all_to_all x0 -> x2, starting transfers between devices: none -> 10.4 us  [the longest x1 7.38 us: spread_rows(): lax.all_to_all(jnp.broadcast_to(own[None], (rows,) + own.shape), 'rows',...]
    all_to_all x0 -> x2, waiting for transfers between devices: none -> 7.72 us  [the longest x1 7.72 us: per_device(): all_stats = lax.all_to_all(stats, ('rows', 'chan'), 0, 0)]
  transfers between devices with their start and end apart: 8 -> 15, of which waited for: 2 -> 3; matrix products, arithmetic and copies ran while one was open for 20% -> 3% of each run, Pallas kernels for 0% -> 15%
where the time goes in v1:
time: 124 us; the launch traced here: 123 us
  starting transfers between devices  33.6 us (27%)
  blocking collectives  32 us (26%)
  Pallas kernels  22.6 us (18%)
  waiting for transfers between devices  20.5 us (17%)
  local copies, waits for them, and re-layouts  14.1 us (11%)
    all_gather x1, blocking collectives, per_device(): lax.all_gather(weight_parts(down_weight), 'rows', axis=0, tiled=False)  32 us
    pallas_call x1, Pallas kernels, per_device(): pl.pallas_call(functools.partial(front_kernel, parts=parts, channels=chan...  18.6 us
    ppermute x7, starting transfers between devices, shifted(): return lax.ppermute(block, axis, route)  15.5 us
    ppermute x6, waiting for transfers between devices, swapped(): lax.ppermute(block, axis, [(i, i ^ bit) for i in range(lax.axis_size(axis...  8.28 us
    ppermute x6, starting transfers between devices, swapped(): lax.ppermute(block, axis, [(i, i ^ bit) for i in range(lax.axis_size(axis...  7.75 us
    all_to_all x1, waiting for transfers between devices, per_device(): all_stats = lax.all_to_all(stats, ('rows', 'chan'), 0, 0)  7.72 us
    all_to_all x1, starting transfers between devices, spread_rows(): lax.all_to_all(jnp.broadcast_to(own[None], (rows,) + own.shape), 'rows',...  7.38 us
    unnamed x18, local copies, waits for them, and re-layouts  7.14 us
  transfers between devices with their start and end apart: 15, of which 3 were waited for; matrix products, arithmetic and copies ran while one was open for 3% of the time, Pallas kernels for 15%

profile of v1, /device:TPU:0, one launch (start us, length us, event | category | flops | bytes accessed | tf_op | source)
XLA Modules:
  0.0 123.2 jit_solution(13105237442653648344)
XLA Ops:
  0.0 0.9 copy-done
  2.4 7.4 %all-to-all-start = ((bf16[8,8,3072]{2,1,0:T(8,128)(2,1)}), bf16[8,8,3072]{2,1,0:T(8,128)(2,1)S(1)}, u32[]{:S(2)}, u32[]{:S(2)}) async-start(bf16[8,8,3072]{2,1,0:T(8,128)(2,1)} %broadcast_in_dim.2), calls=%async_computation | async-start | bytes 786432 | tf_op jit(solution)/shard_map/all_to_all | solution.py:36
  9.8 1.0 fusion
  10.8 1.5 %collective-permute-start.2 = (bf16[9,4,8,256]{3,2,1,0:T(8,128)(2,1)S(1)}, bf16[9,4,8,256]{3,2,1,0:T(8,128)(2,1)S(1)}, u32[]{:S(2)}, u32[]{:S(2)}) collective-permute-start(bf16[9,4,8,256]{3,2,1,0:T(8,128)(2,1)S(1)} %get-tuple-element.14), channel_id=1, source_target_pairs={{0,1},{1,2},{2,3},{4,5},{5,6},{6,7},{8,9},{9,10},{10,11},{12,13},{... | collective-permute-start | bytes 442376 | tf_op jit(solution)/shard_map/ppermute | solution.py:20
  12.3 1.3 %collective-permute-start.3 = (bf16[9,4,8,256]{3,2,1,0:T(8,128)(2,1)S(1)}, bf16[9,4,8,256]{3,2,1,0:T(8,128)(2,1)S(1)}, u32[]{:S(2)}, u32[]{:S(2)}) collective-permute-start(bf16[9,4,8,256]{3,2,1,0:T(8,128)(2,1)S(1)} %get-tuple-element.13), channel_id=1, source_target_pairs={{1,0},{2,1},{3,2},{5,4},{6,5},{7,6},{9,8},{10,9},{11,10},{13,12},{... | collective-permute-start | bytes 442376 | tf_op jit(solution)/shard_map/ppermute | solution.py:20
  13.6 2.3 %fusion.1 = (bf16[9,1,120,256]{3,2,1,0:T(8,128)(2,1)}, bf16[9,1,120,256]{3,2,1,0:T(8,128)(2,1)}) fusion(bf16[9,4,120,256]{3,2,1,0:T(8,128)(2,1)} %frames.1), kind=kLoop, calls=%fused_computation.8 | loop fusion | bytes 2211840 | tf_op jit(solution)/shard_map/slice | solution.py:274
  15.8 4.6 %collective-permute-start = (bf16[9,1,120,256]{3,2,1,0:T(8,128)(2,1)}, bf16[9,1,120,256]{3,2,1,0:T(8,128)(2,1)}, u32[]{:S(2)}, u32[]{:S(2)}) collective-permute-start(bf16[9,1,120,256]{3,2,1,0:T(8,128)(2,1)} %get-tuple-element.16), channel_id=1, source_target_pairs={{0,4},{4,8},{8,12},{12,16},{16,20},{20,24},{24,28},{1,5},{5,9},{9,... | collective-permute-start | bytes 1658888 | tf_op jit(solution)/shard_map/ppermute | solution.py:20
  20.4 1.3 %collective-permute-start.1 = (bf16[9,1,120,256]{3,2,1,0:T(8,128)(2,1)}, bf16[9,1,120,256]{3,2,1,0:T(8,128)(2,1)}, u32[]{:S(2)}, u32[]{:S(2)}) collective-permute-start(bf16[9,1,120,256]{3,2,1,0:T(8,128)(2,1)} %get-tuple-element.15), channel_id=1, source_target_pairs={{4,0},{8,4},{12,8},{16,12},{20,16},{24,20},{28,24},{5,1},{9,5},{13... | collective-permute-start | bytes 1658888 | tf_op jit(solution)/shard_map/ppermute | solution.py:20
  21.7 4.6 %collective-permute-start.7 = (bf16[8,8,3072]{2,1,0:T(8,128)(2,1)S(1)}, bf16[8,8,3072]{2,1,0:T(8,128)(2,1)}, u32[]{:S(2)}, u32[]{:S(2)}) collective-permute-start(bf16[8,8,3072]{2,1,0:T(8,128)(2,1)S(1)} %all-to-all-done.rest_0_), channel_id=1, source_target_pairs={{0,2},{1,3},{2,0},{3,1},{4,6},{5,7},{6,4},{7,5},{8,10},{9,11},{10,... | collective-permute-start | bytes 1179656 | tf_op jit(solution)/shard_map/ppermute | solution.py:24
  27.2 8.3 %collective-permute-done.7.rest_2_ = bf16[8,8,3072]{2,1,0:T(8,128)(2,1)} collective-permute-done((bf16[8,8,3072]{2,1,0:T(8,128)(2,1)S(1)}, bf16[8,8,3072]{2,1,0:T(8,128)(2,1)}, u32[]{:S(2)}, u32[]{:S(2)}) %collective-permute-start.7) | collective-permute-done | bytes 393248 | tf_op jit(solution)/shard_map/ppermute | solution.py:24
  35.5 4.3 %collective-permute-start.4 = (bf16[9,1,8,256]{3,2,1,0:T(8,128)(2,1)S(1)}, bf16[9,1,8,256]{3,2,1,0:T(8,128)(2,1)S(1)}, u32[]{:S(2)}, u32[]{:S(2)}) collective-permute-start(bf16[9,1,8,256]{3,2,1,0:T(8,128)(2,1)S(1)} %get-tuple-element.18), channel_id=1, source_target_pairs={{0,4},{4,8},{8,12},{12,16},{16,20},{20,24},{24,28},{1,5},{5,9},{9,... | collective-permute-start | bytes 110600 | tf_op jit(solution)/shard_map/ppermute | solution.py:20
  39.8 32.0 %all-gather = bf16[64,2304]{1,0:T(8,128)(2,1)S(1)} all-gather(bf16[8,2304]{1,0:T(8,128)(2,1)S(1)} %constant_dynamic-slice_fusion), channel_id=2, replica_groups=mesh['rows'=8,'chan'=4] {'rows'}, dimensions={0}, use_global_device_ids=true | all-gather | bytes 331776 | tf_op jit(solution)/shard_map/all_gather | solution.py:287
  71.8 1.3 %collective-permute-start.5 = (bf16[9,1,8,256]{3,2,1,0:T(8,128)(2,1)S(1)}, bf16[9,1,8,256]{3,2,1,0:T(8,128)(2,1)S(1)}, u32[]{:S(2)}, u32[]{:S(2)}) collective-permute-start(bf16[9,1,8,256]{3,2,1,0:T(8,128)(2,1)S(1)} %get-tuple-element.17), channel_id=1, source_target_pairs={{4,0},{8,4},{12,8},{16,12},{20,16},{24,20},{28,24},{5,1},{9,5},{13... | collective-permute-start | bytes 110600 | tf_op jit(solution)/shard_map/ppermute | solution.py:20
  73.2 4.5 %collective-permute-done.5.pack_bottom = bf16[9,1,8,256]{3,2,1,0:T(8,128)(2,1)S(1)} collective-permute-done((bf16[9,1,8,256]{3,2,1,0:T(8,128)(2,1)S(1)}, bf16[9,1,8,256]{3,2,1,0:T(8,128)(2,1)S(1)}, u32[]{:S(2)}, u32[]{:S(2)}) %collective-permute-start.5) | collective-permute-done | bytes 36896 | tf_op jit(solution)/shard_map/ppermute | solution.py:20
  77.7 2.6 %collective-permute-start.11 = (bf16[8,8,2304]{2,1,0:T(8,128)(2,1)S(1)}, bf16[8,8,2304]{2,1,0:T(8,128)(2,1)S(1)}, u32[]{:S(2)}, u32[]{:S(2)}) collective-permute-start(bf16[8,8,2304]{2,1,0:T(8,128)(2,1)S(1)} %bitcast.8), channel_id=1, source_target_pairs={{0,2},{1,3},{2,0},{3,1},{4,6},{5,7},{6,4},{7,5},{8,10},{9,11},{10,... | collective-permute-start | bytes 884744 | tf_op jit(solution)/shard_map/ppermute | solution.py:24
  80.2 18.6 %front.1 = (bf16[9,128,256]{2,1,0:T(8,128)(2,1)}, f32[9,4,2,128,128]{4,3,2,1,0:T(8,128)S(1)}, f32[32,2,256]{2,1,0:T(2,128)}, bf16[256,768]{1,0:T(8,128)(2,1)S(1)}) custom-call(s32[4]{0:T(128)S(1)} %pad_add_fusion.index, bf16[9,4,120,256]{3,2,1,0:T(8,128)(2,1)S(1)} %copy-done.1, bf16[9,1,120,256]{3,2,1,0:T(8,128)(2,1)} %collective-permute-done.top, ...), custom_call_target="tpu_custom_call" | custom-call | flops 7247757312 | bytes 12582912 | tf_op jit(solution)/shard_map/front/pallas_call | solution.py:304
  98.8 2.1 %copy-done.5 = f32[9,4,2,128,128]{4,3,2,1,0:T(8,128)} copy-done((f32[9,4,2,128,128]{4,3,2,1,0:T(8,128)}, f32[9,4,2,128,128]{4,3,2,1,0:T(8,128)S(1)}, u32[]{:S(2)}) %copy-start.5) | copy-done | bytes 4718616
  101.7 1.3 %collective-permute-start.9 = (bf16[9,128,256]{2,1,0:T(8,128)(2,1)}, bf16[9,128,256]{2,1,0:T(8,128)(2,1)S(1)}, u32[]{:S(2)}, u32[]{:S(2)}) collective-permute-start(bf16[9,128,256]{2,1,0:T(8,128)(2,1)} %get-tuple-element.10), channel_id=1, source_target_pairs={{4,0},{8,4},{12,8},{16,12},{20,16},{24,20},{28,24},{5,1},{9,5},{13... | collective-permute-start | bytes 1769480 | tf_op jit(solution)/shard_map/ppermute | solution.py:20
  103.6 3.0 %all-to-all-start.1 = ((f32[32,2,256]{2,1,0:T(2,128)}), f32[32,2,256]{2,1,0:T(2,128)S(1)}, u32[]{:S(2)}, u32[]{:S(2)}) async-start(f32[32,2,256]{2,1,0:T(2,128)} %get-tuple-element.12), calls=%async_computation.1 | async-start | bytes 131072 | tf_op jit(solution)/shard_map/all_to_all | solution.py:348
  106.7 7.7 %all-to-all-done.1.stats = f32[32,2,256]{2,1,0:T(2,128)S(1)} async-done(((f32[32,2,256]{2,1,0:T(2,128)}), f32[32,2,256]{2,1,0:T(2,128)S(1)}, u32[]{:S(2)}, u32[]{:S(2)}) %all-to-all-start.1) | async-done | bytes 65568 | tf_op jit(solution)/shard_map/all_to_all | solution.py:348
  114.4 2.3 %copy-done.6 = f32[9,4,2,128,128]{4,3,2,1,0:T(8,128)S(1)} copy-done((f32[9,4,2,128,128]{4,3,2,1,0:T(8,128)S(1)}, f32[9,4,2,128,128]{4,3,2,1,0:T(8,128)}, u32[]{:S(2)}) %copy-start.6) | copy-done | bytes 4718616
  116.7 1.0 copy-done.8
  117.7 4.1 %back.1 = bf16[9,2,60,256]{3,2,1,0:T(8,128)(2,1)S(1)} custom-call(s32[4]{0:T(128)S(1)} %pad_add_fusion.index, f32[9,4,2,128,128]{4,3,2,1,0:T(8,128)S(1)} %copy-done.6, bf16[9,128,256]{2,1,0:T(8,128)(2,1)S(1)} %collective-permute-done.9.halo, bf16[256,768]{1,0:T(8,128)(2,1)S(1)} %copy-done.8, f32[32,2,256]{2,1,0:T(2,128)S(1)} %all-to-all-done.1.stats, ...), custom_call_target="tpu_custom_call" | custom-call | flops 1811939328 | bytes 10485760 | tf_op jit(solution)/shard_map/back/pallas_call | solution.py:356
  121.8 1.4 %copy.8 = bf16[9,2,60,256]{3,1,2,0:T(2,128)(2,1)} copy(bf16[9,2,60,256]{3,2,1,0:T(8,128)(2,1)S(1)} %back.1) | data formatting | bytes 1105920 | tf_op jit(solution)/shard_map/back/pallas_call | solution.py:356
  (39 shorter events, 3.9 us)
Async XLA Ops:
  0.0 0.9 copy-start
  2.4 77.8 %copy-start.1 = (bf16[9,4,120,256]{3,2,1,0:T(8,128)(2,1)S(1)}, bf16[9,4,120,256]{3,2,1,0:T(8,128)(2,1)}, u32[]{:S(2)}) copy-start(bf16[9,4,120,256]{3,2,1,0:T(8,128)(2,1)} %frames.1) | copy-start | bytes 6635524
  2.4 19.3 %all-to-all-start = ((bf16[8,8,3072]{2,1,0:T(8,128)(2,1)}), bf16[8,8,3072]{2,1,0:T(8,128)(2,1)S(1)}, u32[]{:S(2)}, u32[]{:S(2)}) async-start(bf16[8,8,3072]{2,1,0:T(8,128)(2,1)} %broadcast_in_dim.2), calls=%async_computation | async-start | bytes 786432 | tf_op jit(solution)/shard_map/all_to_all | solution.py:36
  10.8 16.3 %collective-permute-start.2 = (bf16[9,4,8,256]{3,2,1,0:T(8,128)(2,1)S(1)}, bf16[9,4,8,256]{3,2,1,0:T(8,128)(2,1)S(1)}, u32[]{:S(2)}, u32[]{:S(2)}) collective-permute-start(bf16[9,4,8,256]{3,2,1,0:T(8,128)(2,1)S(1)} %get-tuple-element.14), channel_id=1, source_target_pairs={{0,1},{1,2},{2,3},{4,5},{5,6},{6,7},{8,9},{9,10},{10,11},{12,13},{... | collective-permute-start | bytes 442376 | tf_op jit(solution)/shard_map/ppermute | solution.py:20
  12.3 14.8 %collective-permute-start.3 = (bf16[9,4,8,256]{3,2,1,0:T(8,128)(2,1)S(1)}, bf16[9,4,8,256]{3,2,1,0:T(8,128)(2,1)S(1)}, u32[]{:S(2)}, u32[]{:S(2)}) collective-permute-start(bf16[9,4,8,256]{3,2,1,0:T(8,128)(2,1)S(1)} %get-tuple-element.13), channel_id=1, source_target_pairs={{1,0},{2,1},{3,2},{5,4},{6,5},{7,6},{9,8},{10,9},{11,10},{13,12},{... | collective-permute-start | bytes 442376 | tf_op jit(solution)/shard_map/ppermute | solution.py:20
  15.8 64.4 %collective-permute-start = (bf16[9,1,120,256]{3,2,1,0:T(8,128)(2,1)}, bf16[9,1,120,256]{3,2,1,0:T(8,128)(2,1)}, u32[]{:S(2)}, u32[]{:S(2)}) collective-permute-start(bf16[9,1,120,256]{3,2,1,0:T(8,128)(2,1)} %get-tuple-element.16), channel_id=1, source_target_pairs={{0,4},{4,8},{8,12},{12,16},{16,20},{20,24},{24,28},{1,5},{5,9},{9,... | collective-permute-start | bytes 1658888 | tf_op jit(solution)/shard_map/ppermute | solution.py:20
  20.4 59.8 %collective-permute-start.1 = (bf16[9,1,120,256]{3,2,1,0:T(8,128)(2,1)}, bf16[9,1,120,256]{3,2,1,0:T(8,128)(2,1)}, u32[]{:S(2)}, u32[]{:S(2)}) collective-permute-start(bf16[9,1,120,256]{3,2,1,0:T(8,128)(2,1)} %get-tuple-element.15), channel_id=1, source_target_pairs={{4,0},{8,4},{12,8},{16,12},{20,16},{24,20},{28,24},{5,1},{9,5},{13... | collective-permute-start | bytes 1658888 | tf_op jit(solution)/shard_map/ppermute | solution.py:20
  21.7 13.8 %collective-permute-start.7 = (bf16[8,8,3072]{2,1,0:T(8,128)(2,1)S(1)}, bf16[8,8,3072]{2,1,0:T(8,128)(2,1)}, u32[]{:S(2)}, u32[]{:S(2)}) collective-permute-start(bf16[8,8,3072]{2,1,0:T(8,128)(2,1)S(1)} %all-to-all-done.rest_0_), channel_id=1, source_target_pairs={{0,2},{1,3},{2,0},{3,1},{4,6},{5,7},{6,4},{7,5},{8,10},{9,11},{10,... | collective-permute-start | bytes 1179656 | tf_op jit(solution)/shard_map/ppermute | solution.py:24
  27.2 53.1 %collective-permute-start.6 = (bf16[8,8,3072]{2,1,0:T(8,128)(2,1)S(1)}, bf16[8,8,3072]{2,1,0:T(8,128)(2,1)}, u32[]{:S(2)}, u32[]{:S(2)}) collective-permute-start(bf16[8,8,3072]{2,1,0:T(8,128)(2,1)S(1)} %all-to-all-done.rest_0_), channel_id=1, source_target_pairs={{0,1},{1,0},{2,3},{3,2},{4,5},{5,4},{6,7},{7,6},{8,9},{9,8},{10,11... | collective-permute-start | bytes 1179656 | tf_op jit(solution)/shard_map/ppermute | solution.py:24
  35.5 44.7 %collective-permute-start.8 = (bf16[8,8,3072]{2,1,0:T(8,128)(2,1)}, bf16[8,8,3072]{2,1,0:T(8,128)(2,1)}, u32[]{:S(2)}, u32[]{:S(2)}) collective-permute-start(bf16[8,8,3072]{2,1,0:T(8,128)(2,1)} %collective-permute-done.7.rest_2_), channel_id=1, source_target_pairs={{0,1},{1,0},{2,3},{3,2},{4,5},{5,4},{6,7},{7,6},{8,9},{9,8},{10,11... | collective-permute-start | bytes 1179656 | tf_op jit(solution)/shard_map/ppermute | solution.py:24
  35.5 36.3 %collective-permute-start.4 = (bf16[9,1,8,256]{3,2,1,0:T(8,128)(2,1)S(1)}, bf16[9,1,8,256]{3,2,1,0:T(8,128)(2,1)S(1)}, u32[]{:S(2)}, u32[]{:S(2)}) collective-permute-start(bf16[9,1,8,256]{3,2,1,0:T(8,128)(2,1)S(1)} %get-tuple-element.18), channel_id=1, source_target_pairs={{0,4},{4,8},{8,12},{12,16},{16,20},{20,24},{24,28},{1,5},{5,9},{9,... | collective-permute-start | bytes 110600 | tf_op jit(solution)/shard_map/ppermute | solution.py:20
  71.8 5.8 %collective-permute-start.5 = (bf16[9,1,8,256]{3,2,1,0:T(8,128)(2,1)S(1)}, bf16[9,1,8,256]{3,2,1,0:T(8,128)(2,1)S(1)}, u32[]{:S(2)}, u32[]{:S(2)}) collective-permute-start(bf16[9,1,8,256]{3,2,1,0:T(8,128)(2,1)S(1)} %get-tuple-element.17), channel_id=1, source_target_pairs={{4,0},{8,4},{12,8},{16,12},{20,16},{24,20},{28,24},{5,1},{9,5},{13... | collective-permute-start | bytes 110600 | tf_op jit(solution)/shard_map/ppermute | solution.py:20
  77.7 36.7 %copy-start.2 = (f32[256]{0:T(256)S(1)}, f32[256]{0:T(256)}, u32[]{:S(2)}) copy-start(f32[256]{0:T(256)} %param.11) | copy-start | bytes 3076
  77.7 36.7 %copy-start.3 = (f32[256]{0:T(256)S(1)}, f32[256]{0:T(256)}, u32[]{:S(2)}) copy-start(f32[256]{0:T(256)} %param.12) | copy-start | bytes 3076
  77.7 36.7 %copy-start.4 = (f32[256]{0:T(256)S(1)}, f32[256]{0:T(256)}, u32[]{:S(2)}) copy-start(f32[256]{0:T(256)} %param.13) | copy-start | bytes 3076
  77.7 25.4 %collective-permute-start.11 = (bf16[8,8,2304]{2,1,0:T(8,128)(2,1)S(1)}, bf16[8,8,2304]{2,1,0:T(8,128)(2,1)S(1)}, u32[]{:S(2)}, u32[]{:S(2)}) collective-permute-start(bf16[8,8,2304]{2,1,0:T(8,128)(2,1)S(1)} %bitcast.8), channel_id=1, source_target_pairs={{0,2},{1,3},{2,0},{3,1},{4,6},{5,7},{6,4},{7,5},{8,10},{9,11},{10,... | collective-permute-start | bytes 884744 | tf_op jit(solution)/shard_map/ppermute | solution.py:24
  98.8 2.1 %copy-start.5 = (f32[9,4,2,128,128]{4,3,2,1,0:T(8,128)}, f32[9,4,2,128,128]{4,3,2,1,0:T(8,128)S(1)}, u32[]{:S(2)}) copy-start(f32[9,4,2,128,128]{4,3,2,1,0:T(8,128)S(1)} %get-tuple-element.9.hidden) | copy-start | bytes 14155780
  101.0 0.7 copy-start.7
  101.7 12.7 %collective-permute-start.9 = (bf16[9,128,256]{2,1,0:T(8,128)(2,1)}, bf16[9,128,256]{2,1,0:T(8,128)(2,1)S(1)}, u32[]{:S(2)}, u32[]{:S(2)}) collective-permute-start(bf16[9,128,256]{2,1,0:T(8,128)(2,1)} %get-tuple-element.10), channel_id=1, source_target_pairs={{4,0},{8,4},{12,8},{16,12},{20,16},{24,20},{28,24},{5,1},{9,5},{13... | collective-permute-start | bytes 1769480 | tf_op jit(solution)/shard_map/ppermute | solution.py:20
  103.0 3.6 %collective-permute-start.10 = (bf16[8,8,2304]{2,1,0:T(8,128)(2,1)S(1)}, bf16[8,8,2304]{2,1,0:T(8,128)(2,1)S(1)}, u32[]{:S(2)}, u32[]{:S(2)}) collective-permute-start(bf16[8,8,2304]{2,1,0:T(8,128)(2,1)S(1)} %bitcast.9), channel_id=1, source_target_pairs={{0,1},{1,0},{2,3},{3,2},{4,5},{5,4},{6,7},{7,6},{8,9},{9,8},{10,11... | collective-permute-start | bytes 884744 | tf_op jit(solution)/shard_map/ppermute | solution.py:24
  103.1 3.5 %collective-permute-start.12 = (bf16[8,8,2304]{2,1,0:T(8,128)(2,1)S(1)}, bf16[8,8,2304]{2,1,0:T(8,128)(2,1)S(1)}, u32[]{:S(2)}, u32[]{:S(2)}) collective-permute-start(bf16[8,8,2304]{2,1,0:T(8,128)(2,1)S(1)} %collective-permute-done.11.rest_2_), channel_id=1, source_target_pairs={{0,1},{1,0},{2,3},{3,2},{4,5},{5,4},{6,7},{7,6},{8,9},{9,8},{10,11... | collective-permute-start | bytes 884744 | tf_op jit(solution)/shard_map/ppermute | solution.py:24
  103.6 10.8 %all-to-all-start.1 = ((f32[32,2,256]{2,1,0:T(2,128)}), f32[32,2,256]{2,1,0:T(2,128)S(1)}, u32[]{:S(2)}, u32[]{:S(2)}) async-start(f32[32,2,256]{2,1,0:T(2,128)} %get-tuple-element.12), calls=%async_computation.1 | async-start | bytes 131072 | tf_op jit(solution)/shard_map/all_to_all | solution.py:348
  114.4 2.3 %copy-start.6 = (f32[9,4,2,128,128]{4,3,2,1,0:T(8,128)S(1)}, f32[9,4,2,128,128]{4,3,2,1,0:T(8,128)}, u32[]{:S(2)}) copy-start(f32[9,4,2,128,128]{4,3,2,1,0:T(8,128)} %copy-done.5) | copy-start | bytes 14155780
  116.7 1.0 copy-start.8

commit v2 on v0

v2 whole, which is shorter than its diff:
```python
import functools

import jax
import jax.numpy as jnp
from jax import lax
from jax.experimental import pallas as pl
from jax.experimental.pallas import tpu as pltpu
from jax.sharding import PartitionSpec as P

GROUPS = 32
EPSILON = 1e-06
LANE_COLS = 128
SIDE = 8
GRANT = 56
BATCH = 3
F32 = jnp.float32
BF16 = jnp.bfloat16


def shifted(block, axis, distance):
    count = lax.axis_size(axis)
    return lax.ppermute(block, axis, [(i, (i + distance) % count) for i in range(count)])


def swapped(block, axis, bit):
    return lax.ppermute(block, axis, [(i, i ^ bit) for i in range(lax.axis_size(axis))])


def spread_chan(held):
    parts = {0: held}
    bit = lax.axis_size("chan") // 2
    while bit:
        parts.update({k ^ bit: swapped(part, "chan", bit) for k, part in parts.items()})
        bit //= 2
    return [parts[k] for k in range(len(parts))]


def anywhere(count):
    return [pl.BlockSpec(memory_space=pl.ANY)] * count


def staged_call(body, sources, kept, outs, sems, name):
    return pl.pallas_call(
        body,
        out_shape=outs,
        in_specs=[pl.BlockSpec(memory_space=pltpu.HBM)] * len(sources),
        out_specs=anywhere(len(outs)),
        scratch_shapes=[pltpu.VMEM(k.shape, k.dtype) for k in kept]
        + [pltpu.SemaphoreType.DMA((n,)) for n in sems],
        compiler_params=params(GRANT, grid=0),
        name=name,
    )(*sources)


def side_columns(frames):
    n_frames, rows, cols, channels = frames.shape
    side = jax.ShapeDtypeStruct((n_frames, rows, SIDE, channels), frames.dtype)

    def body(source, first, last, first_kept, last_kept, sems, out_sems):
        moves = [
            (source.at[:, :, 0:SIDE], first_kept, first),
            (source.at[:, :, cols - SIDE :], last_kept, last),
        ]
        fetches = [
            pltpu.make_async_copy(src, hold, sems.at[k])
            for k, (src, hold, _) in enumerate(moves)
        ]
        stores = [
            pltpu.make_async_copy(hold, dst, out_sems.at[k])
            for k, (_, hold, dst) in enumerate(moves)
        ]
        for fetch in fetches:
            fetch.start()
        for fetch, store in zip(fetches, stores):
            fetch.wait()
            store.start()
        for store in stores:
            store.wait()

    return staged_call(body, [frames], [side, side], [side, side], (2, 2), "side_columns")


def weight_pieces(spatial, temporal, down, channels, copies, part):
    width = 3 * channels
    depth = spatial.shape[0]
    tap = jax.ShapeDtypeStruct((depth, width), spatial.dtype)
    own = jax.ShapeDtypeStruct((part, down.shape[1]), down.dtype)
    picks = [
        (n, at) for n, w in enumerate((spatial, temporal)) for at in range(0, w.shape[1], width)
    ]

    def body(*refs):
        taps, down_ref = refs[:2], refs[2]
        outs, kept, (sems, out_sems) = refs[3:5], refs[5:7], refs[7:]
        chan = lax.axis_index("chan")
        for k, (n, at) in enumerate(picks):
            @pl.when(chan == k)
            def _():
                pltpu.make_async_copy(
                    taps[n].at[:, at : at + width], kept[0], sems.at[0]
                ).start()
        rows = down_ref.at[pl.ds(pl.multiple_of(chan * part, part), part)]
        fetches = [
            pltpu.make_async_copy(taps[0].at[:, 0:width], kept[0], sems.at[0]),
            pltpu.make_async_copy(rows, kept[1], sems.at[1]),
        ]
        fetches[1].start()
        stores = []
        for k, fetch in enumerate(fetches):
            fetch.wait()
            for j in range(copies):
                store = pltpu.make_async_copy(
                    kept[k], outs[k].at[j], out_sems.at[len(stores)]
                )
                store.start()
                stores.append(store)
        for store in stores:
            store.wait()

    outs = [jax.ShapeDtypeStruct((copies,) + k.shape, k.dtype) for k in (tap, own)]
    return staged_call(
        body, [spatial, temporal, down], [tap, own], outs, (2, 2 * copies), "weight_pieces"
    )


def extended_kernel(last_row, first_row, left, right, low, high, pack):
    rows, cols = left.shape[1], last_row.shape[2]
    chan = lax.axis_index("chan")
    at = lax.broadcasted_iota(jnp.int32, left.shape, 2)
    before = jnp.where(chan == 0, 0.0, left[...].astype(F32))
    after = jnp.where(chan == lax.axis_size("chan") - 1, 0.0, right[...].astype(F32))
    side = jnp.where(at == SIDE - 1, before, after).astype(BF16)
    pack[...] = side
    low[:, :, :cols] = last_row[...]
    low[:, :, cols:] = side[:, rows - 1 :]
    high[:, :, :cols] = first_row[...]
    high[:, :, cols:] = side[:, :1]


def extended_call(frames, left, right):
    n_frames, rows, cols, channels = frames.shape
    row = (n_frames, 1, cols, channels)
    full = (n_frames, 1, LANE_COLS, channels)
    wide = jax.ShapeDtypeStruct(full, BF16)
    return pl.pallas_call(
        extended_kernel,
        grid=(1,),
        in_specs=[
            pl.BlockSpec(row, lambda i: (0, rows - 1, 0, 0)),
            pl.BlockSpec(row, lambda i: (0, 0, 0, 0)),
            whole(left.shape),
            whole(right.shape),
        ],
        out_specs=[whole(full), whole(full), whole(left.shape)],
        out_shape=[wide, wide, jax.ShapeDtypeStruct(left.shape, BF16)],
        compiler_params=params(16),
        cost_estimate=cost(0, 3),
        name="extended",
    )(frames, frames, left, right)


def repeated(own, copies):
    return jnp.broadcast_to(own[None], (copies,) + own.shape)


def stacked(wide, tap, channels):
    block = wide[..., tap * channels : (tap + 1) * channels]
    return block.reshape(channels, channels).astype(BF16)


def side_shift(product):
    channels = product.shape[1] // 3
    product = product.reshape(-1, LANE_COLS, 3 * channels)
    return (
        product[..., channels : 2 * channels]
        + pltpu.roll(product[..., :channels], 1, 1)
        + pltpu.roll(product[..., 2 * channels :], LANE_COLS - 1, 1)
    )


def build_kernel(frames, pack, top, x):
    cols = frames.shape[2]
    rows = frames.shape[1]
    outside = lax.axis_index("rows") == 0
    zero = jnp.zeros((), BF16)
    x[:, 0:1] = jnp.where(outside, zero, top[...])
    x[:, 1 : rows + 1, :cols] = frames[...]
    x[:, 1 : rows + 1, cols:] = pack[...]


def build_call(frames, pack, top):
    n_frames, rows, cols, channels = frames.shape
    batch = 3 if n_frames % 3 == 0 else 1
    shape = (n_frames, rows + 1, LANE_COLS, channels)
    return pl.pallas_call(
        build_kernel,
        grid=(n_frames // batch,),
        in_specs=[
            by_frame(rows, cols, channels, batch=batch),
            by_frame(rows, SIDE, channels, batch=batch),
            by_frame(1, LANE_COLS, channels, batch=batch),
        ],
        out_specs=by_frame(*shape[1:], batch=batch),
        out_shape=jax.ShapeDtypeStruct(shape, BF16),
        compiler_params=params(16),
        cost_estimate=cost(30 << 30, 64),
        name="build",
    )(frames, pack, top)


def inner_kernel(x, *rest, split):
    part_refs = rest[:4]
    first_row, middle, border, weight = rest[4:]
    n_frames, rows, _, channels = x.shape
    rows = rows - 1
    chan = lax.axis_index("chan") if split else 0
    for k, part in enumerate(part_refs):
        weight[chan ^ k] = part[...]

    def conv(f, many, row, count, taps):
        lhs = jnp.concatenate(
            [
                x[pl.ds(f, many), row + a : row + a + count].reshape(-1, channels)
                for a in range(taps)
            ],
            axis=1,
        )
        kernel = weight[:taps].reshape(taps * channels, 3 * channels)
        return side_shift(jnp.dot(lhs, kernel, preferred_element_type=F32))

    many = BATCH if n_frames % BATCH == 0 else 1

    def frames(g, _):
        at = pl.ds(g * many, many)
        first = conv(g * many, many, 0, rows - 1, 3).astype(BF16)
        first = first.reshape(many, rows - 1, LANE_COLS, channels)
        first_row[at] = first[:, 0]
        middle[at] = first.reshape(many, -1, channels)
        border[at] = conv(g * many, many, rows - 1, 1, 2)
        return 0

    lax.fori_loop(0, n_frames // many, frames, 0, unroll=True)


def outer_kernel(
    bottom, middle, border, weight, hidden, stats, temporal, firsts, *, cols
):
    n_frames, channels = middle.shape[0], middle.shape[2]
    rows = middle.shape[1] // LANE_COLS + 1
    size = rows * LANE_COLS
    count = float(rows * cols)
    outside = lax.axis_index("rows") == lax.axis_size("rows") - 1
    for k in range(3):
        at = k * channels
        temporal[at : at + channels] = weight[3, :, at : at + channels]

    many = BATCH if n_frames % BATCH == 0 else 1

    def frames(g, moments):
        mean_all, spread_all = moments
        start = g * many
        at = pl.ds(start, many)
        lhs = bottom[at].reshape(-1, channels)
        lhs = jnp.where(outside, jnp.zeros((), BF16), lhs)
        product = jnp.dot(lhs, weight[2], preferred_element_type=F32)
        last = (side_shift(product) + border[at]).astype(BF16)
        firsts[pl.ds(start + 2, many), : size - LANE_COLS] = middle[at]
        firsts[pl.ds(start + 2, many), size - LANE_COLS :] = last

        @pl.when(g == 0)
        def _():
            firsts[0] = firsts[2]
            firsts[1] = firsts[2]

        lhs = jnp.concatenate(
            [firsts[pl.ds(start + k, many)].reshape(-1, channels) for k in range(3)],
            axis=1,
        )
        total = jnp.dot(lhs, temporal[...], preferred_element_type=F32)
        total = total.reshape(many, rows, LANE_COLS, channels)
        for k in range(channels // 128):
            hidden[at, :, k] = total[..., k * 128 : (k + 1) * 128]
        inner = total[:, :, :cols].reshape(-1, 8, channels)
        mean = jnp.sum(jnp.sum(inner, axis=0), axis=0, keepdims=True) / (count * many)
        spread = jnp.sum(jnp.sum(jnp.square(inner - mean), axis=0), axis=0, keepdims=True)
        done = jnp.asarray(g, jnp.int32).astype(F32)
        delta = mean - mean_all
        mean_all = mean_all + delta / (done + 1.0)
        spread_all = spread_all + spread + delta * delta * (count * many * done / (done + 1.0))
        return mean_all, spread_all

    zero = jnp.zeros((1, channels), F32)
    mean, spread = lax.fori_loop(
        0, n_frames // many, frames, (zero, zero), unroll=True
    )
    stats[...] = jnp.broadcast_to(jnp.concatenate([mean, spread], axis=0)[None], stats.shape)


def back_kernel(
    hidden, halo, temporal, stats, gain, shift, bias, *rest, parts, cols
):
    part_refs = rest[:parts]
    latent, wide, weight, full, even, odd = rest[parts:]
    n_frames, rows, blocks = hidden.shape[:3]
    channels = halo.shape[2]
    half = LANE_COLS // 2
    cols_out = cols // 2
    rows_out = rows // 2
    count = float(n_frames * rows * cols)
    chan = lax.axis_index("chan") if parts > 1 else 0
    last_row = lax.axis_index("rows") == lax.axis_size("rows") - 1
    last_chan = lax.axis_index("chan") == lax.axis_size("chan") - 1

    for k, part in enumerate(part_refs):
        wide[:, chan ^ k] = part[...].astype(F32)
    for a in range(3):
        for b in range(3):
            at = (a + 3 * b) * channels
            weight[at : at + channels] = stacked(wide, 3 * a + b, channels)
    devices = stats.shape[0]
    group = channels // GROUPS
    means = stats[:, 0]
    mean = jnp.sum(means, axis=0, keepdims=True) / float(devices)
    spread = jnp.sum(stats[:, 1], axis=0, keepdims=True) + count * jnp.sum(
        jnp.square(means - mean), axis=0, keepdims=True
    )
    lane = lax.broadcasted_iota(jnp.int32, (channels, channels), 0) // group
    same = lane == lax.broadcasted_iota(jnp.int32, (channels, channels), 1) // group
    same = same.astype(F32)

    def over_group(values):
        return jnp.dot(
            jnp.broadcast_to(values, (8, channels)),
            same,
            precision=lax.Precision.HIGHEST,
            preferred_element_type=F32,
        )[0:1] / float(group)

    mean_group = over_group(mean)
    total = over_group(spread / (count * devices) + jnp.square(mean - mean_group))
    rstd = lax.rsqrt(total + EPSILON)

    def activated(values):
        return jax.nn.silu((values - mean_group) * rstd * gain[...] + shift[...])

    many = BATCH if n_frames % BATCH == 0 else 1
    size = rows_out * many * half
    starts = (0, rows_out + 1, 1)

    def frames(g, _):
        for i in range(many):
            f = g * many + i
            lhs = jnp.concatenate(
                [halo[jnp.maximum(f - 2, 0)], halo[jnp.maximum(f - 1, 0)], halo[f]], axis=1
            )
            extra = jnp.dot(lhs, temporal[...], preferred_element_type=F32)
            for k in range(blocks):
                full[i, k] = extra[:, k * 128 : (k + 1) * 128]

            def columns(row, start):
                picked = pl.ds(start, half, stride=2)
                return jnp.concatenate(
                    [
                        hidden[f, row, k, picked] if row < rows else full[i, k, picked]
                        for k in range(blocks)
                    ],
                    axis=1,
                )

            for row in range(rows + 1):
                place = row // 2 if row % 2 == 0 else rows_out + 1 + row // 2
                e = activated(columns(row, 0))
                o = activated(columns(row, 1))
                at = lax.broadcasted_iota(jnp.int32, e.shape, 0)
                drop = last_chan & (at >= cols_out)
                if row == rows:
                    drop = drop | last_row
                    o = jnp.where(last_row, 0.0, o)
                even[place, i] = jnp.where(drop, 0.0, e).astype(BF16)
                odd[place, i] = o.astype(BF16)
        evens = [even[s : s + rows_out].reshape(size, channels) for s in starts]
        odds = [odd[s : s + rows_out].reshape(size, channels) for s in starts]
        near = jnp.dot(
            jnp.concatenate(evens + odds, axis=1),
            weight[: 6 * channels],
            preferred_element_type=F32,
        )
        far = jnp.dot(
            jnp.concatenate(evens, axis=1),
            weight[6 * channels :],
            preferred_element_type=F32,
        )
        far = far.reshape(rows_out * many, half, channels)
        out = near.reshape(far.shape) + pltpu.roll(far, half - 1, 1) + bias[...]
        out = out.reshape(rows_out, many, half, channels).astype(BF16)
        for p in range(rows_out):
            for i in range(many):
                latent[g * many + i, p] = out[p, i, :cols_out]
        return 0

    lax.fori_loop(0, n_frames // many, frames, 0, unroll=True)


def whole(shape):
    return pl.BlockSpec(shape, lambda i, *_: (0,) * len(shape))


def by_frame(*tail, batch=1):
    return pl.BlockSpec((batch,) + tail, lambda i, *_: (i,) + (0,) * len(tail))


def params(mebibytes, grid=1):
    return pltpu.CompilerParams(
        dimension_semantics=("arbitrary",) * grid, vmem_limit_bytes=mebibytes << 20
    )


def cost(flops, mebibytes, exps=0):
    return pl.CostEstimate(
        flops=flops, bytes_accessed=mebibytes << 20, transcendentals=exps
    )


def in_vmem(count):
    return [pl.BlockSpec(memory_space=pltpu.VMEM)] * count


def inner_call(x, front_parts, split):
    n_frames, rows, _, channels = x.shape
    rows = rows - 1
    tap = 2 * n_frames * LANE_COLS * channels * channels
    return pl.pallas_call(
        functools.partial(inner_kernel, split=split),
        in_specs=in_vmem(5),
        out_specs=in_vmem(4),
        out_shape=[
            jax.ShapeDtypeStruct((n_frames, LANE_COLS, channels), BF16),
            jax.ShapeDtypeStruct((n_frames, (rows - 1) * LANE_COLS, channels), BF16),
            jax.ShapeDtypeStruct((n_frames, LANE_COLS, channels), F32),
            jax.ShapeDtypeStruct((4, channels, 3 * channels), BF16),
        ],
        compiler_params=params(24, grid=0),
        cost_estimate=cost(33 * tap, 8),
        name="inner",
    )(x, *front_parts)


def outer_call(bottom, middle, border, weight, cols, devices):
    n_frames, size, channels = middle.shape
    rows = size // LANE_COLS + 1
    tap = 2 * n_frames * LANE_COLS * channels * channels
    return pl.pallas_call(
        functools.partial(outer_kernel, cols=cols),
        in_specs=in_vmem(4),
        out_specs=in_vmem(3),
        scratch_shapes=[pltpu.VMEM((n_frames + 2, rows * LANE_COLS, channels), BF16)],
        out_shape=[
            pltpu.VMEM((n_frames, rows, channels // 128, LANE_COLS, 128), F32),
            jax.ShapeDtypeStruct((devices, 2, channels), F32),
            pltpu.VMEM((3 * channels, channels), BF16),
        ],
        compiler_params=params(24, grid=0),
        cost_estimate=cost(15 * tap, 10),
        name="outer",
    )(bottom, middle, border, weight)


def back_call(hidden, halo, temporal, all_stats, vectors, back_parts, cols):
    n_frames, rows = hidden.shape[:2]
    channels = halo.shape[2]
    parts = len(back_parts)
    piece = back_parts[0].shape
    many = BATCH if n_frames % BATCH == 0 else 1
    tap = 2 * n_frames * LANE_COLS * channels * channels
    half = LANE_COLS // 2
    return pl.pallas_call(
        functools.partial(back_kernel, parts=parts, cols=cols),
        in_specs=in_vmem(7 + parts),
        out_specs=pl.BlockSpec(memory_space=pltpu.VMEM),
        scratch_shapes=[
            pltpu.VMEM((piece[0], parts, piece[1], piece[2]), F32),
            pltpu.VMEM((9 * channels, channels), BF16),
            pltpu.VMEM((many, channels // 128, LANE_COLS, 128), F32),
            pltpu.VMEM((rows + 1, many, half, channels), BF16),
            pltpu.VMEM((rows + 1, many, half, channels), BF16),
        ],
        out_shape=jax.ShapeDtypeStruct((n_frames, rows // 2, cols // 2, channels), BF16),
        compiler_params=params(24, grid=0),
        cost_estimate=cost(12 * tap, 10, 4 << 20),
        name="back",
    )(hidden, halo, temporal, all_stats, *vectors, *back_parts)


def per_device(
    frames, spatial_weight, temporal_weight, down_weight, norm_gain, norm_shift, down_bias
):
    n_frames, rows, cols, channels = frames.shape
    row_devices, chan_devices = lax.axis_size("rows"), lax.axis_size("chan")
    part = spatial_weight.shape[0] // chan_devices
    split = part % 8 == 0 and chan_devices == 4
    first_cols, last_cols = side_columns(frames)
    right = shifted(first_cols, "chan", -1)
    left = shifted(last_cols, "chan", 1)
    low_row, high_row, pack = extended_call(frames, left, right)
    top = shifted(low_row, "rows", 1)

    if split:
        taps, own = weight_pieces(
            spatial_weight, temporal_weight, down_weight, channels, row_devices, part
        )
        taps = lax.all_to_all(taps, "rows", 0, 0)
        taps, pack = lax.optimization_barrier((taps, pack))
        bottom = shifted(high_row, "rows", -1)
        front_parts = spread_chan(taps.reshape(channels, 3 * channels))
        own, taps = lax.optimization_barrier((own, taps))
        own = lax.all_to_all(own, "rows", 0, 0)
    else:
        bottom = shifted(high_row, "rows", -1)
        joint = jnp.concatenate([spatial_weight, temporal_weight], 1)
        taps = lax.all_gather(joint, "rows", axis=0, tiled=True)
        width = 3 * channels
        front_parts = [taps[:, k * width : (k + 1) * width] for k in range(4)]
        own = lax.all_gather(down_weight, "rows", axis=0, tiled=True)

    x = build_call(frames, pack, top)
    x, own = lax.optimization_barrier((x, own))
    across = swapped(own, "chan", 2) if split else own
    first_row, middle, border, weight = inner_call(x, front_parts, split)
    halo = shifted(first_row, "rows", -1)
    if split:
        own, across, middle = lax.optimization_barrier((own, across, middle))
        back_parts = [own, swapped(own, "chan", 1), across, swapped(across, "chan", 1)]
    else:
        back_parts = [own.reshape(channels // 8, 8, -1)]
    hidden, stats, temporal = outer_call(
        bottom, middle, border, weight, cols, row_devices * chan_devices
    )
    stats, back_parts = lax.optimization_barrier((stats, back_parts))
    all_stats = lax.all_to_all(stats, ("rows", "chan"), 0, 0)
    vectors = [v.reshape(1, channels) for v in (norm_gain, norm_shift, down_bias)]
    return back_call(hidden, halo, temporal, all_stats, vectors, back_parts, cols)


def solution(mesh):
    placed = (
        P(None, "rows", "chan", None),
        P("rows", None),
        P("rows", None),
        P("rows", None),
        P(),
        P(),
        P(),
    )
    return jax.shard_map(
        per_device,
        mesh=mesh,
        in_specs=placed,
        out_specs=P(None, "rows", "chan", None),
        check_vma=False,
    )
```

time: 322 us -> 87.7 us (0.27)
  blocking collectives: 114 us -> 9.12 us
  local copies, waits for them, and re-layouts: 76.4 us -> 6.37 us
  matrix products: 56 us -> 0 us
  Pallas kernels: 0 us -> 20.3 us
  between operations: 13.8 us -> 0.12 us
  starting transfers between devices: 12.3 us -> 25.8 us
  other arithmetic: 10.5 us -> 0 us
  waiting for transfers between devices: 35.5 us -> 25.4 us
    psum x2 -> x0, blocking collectives: 80.5 us -> none  [group_reduce(): return lax.psum(partial_sums, ('rows', 'chan'))]
    slice x17 -> x0, local copies, waits for them, and re-layouts: 67.9 us -> none  [the longest x9 63.3 us: down_taps(): extended[:, row_offset:row_offset + 2 * rows_out:2, col_offset:col_offset...]
    dot_general x21 -> x0, matrix products: 56 us -> none  [the longest x9 36.4 us: spatial_taps(): jnp.einsum('fijc,co->fijo', window, weight_panel, preferred_element_type=...]
    all_gather x1 -> x0, blocking collectives: 33.7 us -> none  [per_device(): lax.all_gather(temporal_weight, 'rows', axis=0, tiled=True)]
    pallas_call x0 -> x7, Pallas kernels: none -> 20.3 us  [the longest x1 6.57 us: inner_call(): pl.pallas_call(functools.partial(inner_kernel, split=split), in_specs=in_...]
    all_to_all x0 -> x2, starting transfers between devices: none -> 10.7 us  [the longest x1 7.26 us: per_device(): taps = lax.all_to_all(taps, 'rows', 0, 0)]
    ppermute x6 -> x11, waiting for transfers between devices: 34.7 us -> 24.5 us  [the longest x5 20.7 us: shifted(): lax.ppermute(block, axis, [(i, (i + distance) % count) for i in range(cou...]
    all_to_all x0 -> x1, blocking collectives: none -> 9.12 us  [per_device(): all_stats = lax.all_to_all(stats, ('rows', 'chan'), 0, 0)]
  transfers between devices with their start and end apart: 8 -> 13, of which waited for: 2 -> 5; matrix products, arithmetic and copies ran while one was open for 20% -> 0% of each run, Pallas kernels for 0% -> 18%
where the time goes in v2:
time: 87.7 us; the launch traced here: 87.2 us
  starting transfers between devices  25.8 us (29%)
  waiting for transfers between devices  25.4 us (29%)
  Pallas kernels  20.3 us (23%)
  blocking collectives  9.12 us (10%)
  local copies, waits for them, and re-layouts  6.37 us (7%)
    ppermute x5, waiting for transfers between devices, shifted(): lax.ppermute(block, axis, [(i, (i + distance) % count) for i in range(cou...  20.7 us
    ppermute x5, starting transfers between devices, shifted(): lax.ppermute(block, axis, [(i, (i + distance) % count) for i in range(cou...  11.4 us
    all_to_all x1, blocking collectives, per_device(): all_stats = lax.all_to_all(stats, ('rows', 'chan'), 0, 0)  9.12 us
    all_to_all x1, starting transfers between devices, per_device(): taps = lax.all_to_all(taps, 'rows', 0, 0)  7.26 us
    pallas_call x1, Pallas kernels, inner_call(): pl.pallas_call(functools.partial(inner_kernel, split=split), in_specs=in_...  6.57 us
    unnamed x16, local copies, waits for them, and re-layouts  5 us
    pallas_call x1, Pallas kernels, outer_call(): pl.pallas_call(functools.partial(outer_kernel, cols=cols), in_specs=in_vm...  4.31 us
    ppermute x6, waiting for transfers between devices, swapped(): lax.ppermute(block, axis, [(i, i ^ bit) for i in range(lax.axis_size(axis...  3.83 us
  transfers between devices with their start and end apart: 13, of which 5 were waited for; matrix products, arithmetic and copies ran while one was open for 0% of the time, Pallas kernels for 18%

profile of v2, /device:TPU:0, one launch (start us, length us, event | category | flops | bytes accessed | tf_op | source)
XLA Modules:
  0.0 87.2 jit_solution(11816468475158329075)
XLA Ops:
  0.0 1.9 %weight_pieces.1 = (bf16[8,32,768]{2,1,0:T(8,128)(2,1)}, bf16[8,8,2304]{2,1,0:T(8,128)(2,1)}) custom-call(bf16[32,2304]{1,0:T(8,128)(2,1)} %refs_0_.1, bf16[32,768]{1,0:T(8,128)(2,1)} %refs_1_.1, bf16[32,2304]{1,0:T(8,128)(2,1)} %refs_2_.1), custom_call_target="tpu_custom_call" | custom-call | tf_op jit(solution)/shard_map/weight_pieces/pallas_call | solution.py:43
  1.9 7.3 %all-to-all-start = ((bf16[8,32,768]{2,1,0:T(8,128)(2,1)}), bf16[8,32,768]{2,1,0:T(8,128)(2,1)S(1)}, u32[]{:S(2)}, u32[]{:S(2)}) async-start(bf16[8,32,768]{2,1,0:T(8,128)(2,1)} %get-tuple-element.35), calls=%async_computation | async-start | bytes 786432 | tf_op jit(solution)/shard_map/all_to_all | solution.py:511
  9.2 1.7 %side_columns.1 = (bf16[9,4,8,256]{3,2,1,0:T(8,128)(2,1)}, bf16[9,4,8,256]{3,2,1,0:T(8,128)(2,1)}) custom-call(bf16[9,4,120,256]{3,2,1,0:T(8,128)(2,1)} %frames.1), custom_call_target="tpu_custom_call" | custom-call | tf_op jit(solution)/shard_map/side_columns/pallas_call | solution.py:43
  10.9 1.7 %collective-permute-start.1 = (bf16[9,4,8,256]{3,2,1,0:T(8,128)(2,1)}, bf16[9,4,8,256]{3,2,1,0:T(8,128)(2,1)S(1)}, u32[]{:S(2)}, u32[]{:S(2)}) collective-permute-start(bf16[9,4,8,256]{3,2,1,0:T(8,128)(2,1)} %get-tuple-element.33), channel_id=1, source_target_pairs={{0,3},{1,0},{2,1},{3,2},{4,7},{5,4},{6,5},{7,6},{8,11},{9,8},{10,9... | collective-permute-start | bytes 442376 | tf_op jit(solution)/shard_map/ppermute | solution.py:22
  12.7 3.0 %collective-permute-done.left = bf16[9,4,8,256]{3,2,1,0:T(8,128)(2,1)S(1)} collective-permute-done((bf16[9,4,8,256]{3,2,1,0:T(8,128)(2,1)}, bf16[9,4,8,256]{3,2,1,0:T(8,128)(2,1)S(1)}, u32[]{:S(2)}, u32[]{:S(2)}) %collective-permute-start) | collective-permute-done | bytes 147488 | tf_op jit(solution)/shard_map/ppermute | solution.py:22
  16.4 0.9 %extended.1 = (bf16[9,1,128,256]{3,2,1,0:T(8,128)(2,1)}, bf16[9,1,128,256]{3,2,1,0:T(8,128)(2,1)S(1)}, bf16[9,4,8,256]{3,2,1,0:T(8,128)(2,1)S(1)}) custom-call(bf16[9,4,120,256]{3,2,1,0:T(8,128)(2,1)S(1)} %copy-done, bf16[9,4,120,256]{3,2,1,0:T(8,128)(2,1)S(1)} %copy-done, bf16[9,4,8,256]{3,2,1,0:T(8,128)(2,1)S(1)} %collective-permute-done.left, ...), custom_call_target="tpu_custom_call" | custom-call | bytes 3145728 | tf_op jit(solution)/shard_map/extended/pallas_call | solution.py:145
  18.0 2.0 %collective-permute-start.3 = (bf16[9,1,128,256]{3,2,1,0:T(8,128)(2,1)}, bf16[9,1,128,256]{3,2,1,0:T(8,128)(2,1)}, u32[]{:S(2)}, u32[]{:S(2)}) collective-permute-start(bf16[9,1,128,256]{3,2,1,0:T(8,128)(2,1)} %get-tuple-element.38), channel_id=1, source_target_pairs={{0,4},{4,8},{8,12},{12,16},{16,20},{20,24},{24,28},{28,0},{1,5},{5... | collective-permute-start | bytes 1769480 | tf_op jit(solution)/shard_map/ppermute | solution.py:22
  20.1 0.8 all-to-all-done
  20.9 1.5 %collective-permute-start.6 = (bf16[256,768]{1,0:T(8,128)(2,1)S(1)}, bf16[256,768]{1,0:T(8,128)(2,1)}, u32[]{:S(2)}, u32[]{:S(2)}) collective-permute-start(bf16[256,768]{1,0:T(8,128)(2,1)S(1)} %bitcast.4), channel_id=1, source_target_pairs={{0,2},{1,3},{2,0},{3,1},{4,6},{5,7},{6,4},{7,5},{8,10},{9,11},{10,... | collective-permute-start | bytes 1179656 | tf_op jit(solution)/shard_map/ppermute | solution.py:26
  22.4 2.3 %collective-permute-start.2 = (bf16[9,1,128,256]{3,2,1,0:T(8,128)(2,1)S(1)}, bf16[9,1,128,256]{3,2,1,0:T(8,128)(2,1)}, u32[]{:S(2)}, u32[]{:S(2)}) collective-permute-start(bf16[9,1,128,256]{3,2,1,0:T(8,128)(2,1)S(1)} %get-tuple-element.34), channel_id=1, source_target_pairs={{0,28},{4,0},{8,4},{12,8},{16,12},{20,16},{24,20},{28,24},{1,29},{... | collective-permute-start | bytes 1769480 | tf_op jit(solution)/shard_map/ppermute | solution.py:22
  24.8 3.4 %all-to-all-start.1 = ((bf16[8,8,2304]{2,1,0:T(8,128)(2,1)}), bf16[8,8,2304]{2,1,0:T(8,128)(2,1)S(1)}, u32[]{:S(2)}, u32[]{:S(2)}) async-start(bf16[8,8,2304]{2,1,0:T(8,128)(2,1)} %get-tuple-element.41), calls=%async_computation.1 | async-start | bytes 589824 | tf_op jit(solution)/shard_map/all_to_all | solution.py:516
  28.2 3.8 %collective-permute-done.6.rest_2_ = bf16[256,768]{1,0:T(8,128)(2,1)} collective-permute-done((bf16[256,768]{1,0:T(8,128)(2,1)S(1)}, bf16[256,768]{1,0:T(8,128)(2,1)}, u32[]{:S(2)}, u32[]{:S(2)}) %collective-permute-start.6) | collective-permute-done | bytes 393248 | tf_op jit(solution)/shard_map/ppermute | solution.py:26
  32.0 17.0 %collective-permute-done.3.top = bf16[9,1,128,256]{3,2,1,0:T(8,128)(2,1)} collective-permute-done((bf16[9,1,128,256]{3,2,1,0:T(8,128)(2,1)}, bf16[9,1,128,256]{3,2,1,0:T(8,128)(2,1)}, u32[]{:S(2)}, u32[]{:S(2)}) %collective-permute-start.3) | collective-permute-done | bytes 589856 | tf_op jit(solution)/shard_map/ppermute | solution.py:22
  49.0 0.9 %copy-done.2 = bf16[9,4,8,256]{3,2,1,0:T(8,128)(2,1)S(1)} copy-done((bf16[9,4,8,256]{3,2,1,0:T(8,128)(2,1)S(1)}, bf16[9,4,8,256]{3,2,1,0:T(8,128)(2,1)}, u32[]{:S(2)}) %copy-start.2) | copy-done | bytes 147480
  49.9 2.0 %build.1.x = bf16[9,5,128,256]{3,2,1,0:T(8,128)(2,1)S(1)} custom-call(bf16[9,4,120,256]{3,2,1,0:T(8,128)(2,1)S(1)} %copy-done, bf16[9,4,8,256]{3,2,1,0:T(8,128)(2,1)S(1)} %copy-done.2, bf16[9,1,128,256]{3,2,1,0:T(8,128)(2,1)} %collective-permute-done.3.top), custom_call_target="tpu_custom_call" | custom-call | flops 32212254720 | bytes 67108864 | tf_op jit(solution)/shard_map/build/pallas_call | solution.py:195
  51.9 1.6 %copy-done.6 = bf16[9,5,128,256]{3,2,1,0:T(8,128)(2,1)} copy-done((bf16[9,5,128,256]{3,2,1,0:T(8,128)(2,1)}, bf16[9,5,128,256]{3,2,1,0:T(8,128)(2,1)S(1)}, u32[]{:S(2)}) %copy-start.6) | copy-done | bytes 2949144
  53.5 1.7 %collective-permute-start.4 = (bf16[8,8,2304]{2,1,0:T(8,128)(2,1)S(1)}, bf16[8,8,2304]{2,1,0:T(8,128)(2,1)S(1)}, u32[]{:S(2)}, u32[]{:S(2)}) collective-permute-start(bf16[8,8,2304]{2,1,0:T(8,128)(2,1)S(1)} %all-to-all-done.1.rest_0_), channel_id=1, source_target_pairs={{0,2},{1,3},{2,0},{3,1},{4,6},{5,7},{6,4},{7,5},{8,10},{9,11},{10,... | collective-permute-start | bytes 884744 | tf_op jit(solution)/shard_map/ppermute | solution.py:26
  55.2 1.8 %copy-done.7 = bf16[9,5,128,256]{3,2,1,0:T(8,128)(2,1)S(1)} copy-done((bf16[9,5,128,256]{3,2,1,0:T(8,128)(2,1)S(1)}, bf16[9,5,128,256]{3,2,1,0:T(8,128)(2,1)}, u32[]{:S(2)}) %copy-start.7) | copy-done | bytes 2949144
  57.1 6.6 %inner.1 = (bf16[9,128,256]{2,1,0:T(8,128)(2,1)S(1)}, bf16[9,384,256]{2,1,0:T(8,128)(2,1)S(1)}, f32[9,128,256]{2,1,0:T(8,128)S(1)}, bf16[4,256,768]{2,1,0:T(8,128)(2,1)S(1)}) custom-call(bf16[9,5,128,256]{3,2,1,0:T(8,128)(2,1)S(1)} %copy-done.7, bf16[256,768]{1,0:T(8,128)(2,1)S(1)} %bitcast.6, bf16[256,768]{1,0:T(8,128)(2,1)} %collective-permute-done.5.rest_1_, ...), custom_call_target="tpu_custom_call" | custom-call | flops 4982833152 | bytes 8388608 | tf_op jit(solution)/shard_map/inner/pallas_call | solution.py:432
  63.7 5.2 %collective-permute-start.8 = (bf16[9,128,256]{2,1,0:T(8,128)(2,1)S(1)}, bf16[9,128,256]{2,1,0:T(8,128)(2,1)S(1)}, u32[]{:S(2)}, u32[]{:S(2)}) collective-permute-start(bf16[9,128,256]{2,1,0:T(8,128)(2,1)S(1)} %get-tuple-element.49), channel_id=1, source_target_pairs={{0,28},{4,0},{8,4},{12,8},{16,12},{20,16},{24,20},{28,24},{1,29},{... | collective-permute-start | bytes 1769480 | tf_op jit(solution)/shard_map/ppermute | solution.py:22
  69.4 4.3 %outer.1 = (f32[9,4,2,128,128]{4,3,2,1,0:T(8,128)S(1)}, f32[32,2,256]{2,1,0:T(2,128)S(1)}, bf16[768,256]{1,0:T(8,128)(2,1)S(1)}) custom-call(bf16[9,1,128,256]{3,2,1,0:T(8,128)(2,1)} %collective-permute-done.2.bottom, bf16[9,384,256]{2,1,0:T(8,128)(2,1)S(1)} %get-tuple-element.45.middle, f32[9,128,256]{2,1,0:T(8,128)S(1)} %get-tuple-element.46.border, ...), custom_call_target="tpu_custom_call" | custom-call | flops 2264924160 | bytes 10485760 | tf_op jit(solution)/shard_map/outer/pallas_call | solution.py:452
  73.8 9.1 %all_to_all.15.stats = f32[32,2,256]{2,1,0:T(2,128)S(1)} all-to-all(f32[32,2,256]{2,1,0:T(2,128)S(1)} %get-tuple-element.54), channel_id=1, replica_groups=mesh['rows'=8,'chan'=4] {'rows','chan'}, dimensions={0} | all-to-all | bytes 131072 | tf_op jit(solution)/shard_map/all_to_all | solution.py:539
  82.9 2.9 %back.1 = bf16[9,2,60,256]{3,2,1,0:T(8,128)(2,1)S(1)} custom-call(f32[9,4,2,128,128]{4,3,2,1,0:T(8,128)S(1)} %get-tuple-element.48.hidden, bf16[9,128,256]{2,1,0:T(8,128)(2,1)S(1)} %collective-permute-done.8.halo, bf16[768,256]{1,0:T(8,128)(2,1)S(1)} %get-tuple-element.50.temporal, f32[32,2,256]{2,1,0:T(2,128)S(1)} %all_to_all.15.stats, ...), custom_call_target="tpu_custom_call" | custom-call | flops 1811939328 | bytes 10485760 | tf_op jit(solution)/shard_map/back/pallas_call | solution.py:476
  85.8 1.4 %copy.8 = bf16[9,2,60,256]{3,1,2,0:T(2,128)(2,1)} copy(bf16[9,2,60,256]{3,2,1,0:T(8,128)(2,1)S(1)} %back.1) | data formatting | bytes 1105920 | tf_op jit(solution)/shard_map/back/pallas_call | solution.py:476
  (27 shorter events, 2.0 us)
Async XLA Ops:
  0.0 16.4 %copy-start = (bf16[9,4,120,256]{3,2,1,0:T(8,128)(2,1)S(1)}, bf16[9,4,120,256]{3,2,1,0:T(8,128)(2,1)}, u32[]{:S(2)}) copy-start(bf16[9,4,120,256]{3,2,1,0:T(8,128)(2,1)} %frames.1) | copy-start | bytes 6635524
  1.9 19.0 %all-to-all-start = ((bf16[8,32,768]{2,1,0:T(8,128)(2,1)}), bf16[8,32,768]{2,1,0:T(8,128)(2,1)S(1)}, u32[]{:S(2)}, u32[]{:S(2)}) async-start(bf16[8,32,768]{2,1,0:T(8,128)(2,1)} %get-tuple-element.35), calls=%async_computation | async-start | bytes 786432 | tf_op jit(solution)/shard_map/all_to_all | solution.py:511
  10.9 4.8 %collective-permute-start = (bf16[9,4,8,256]{3,2,1,0:T(8,128)(2,1)}, bf16[9,4,8,256]{3,2,1,0:T(8,128)(2,1)S(1)}, u32[]{:S(2)}, u32[]{:S(2)}) collective-permute-start(bf16[9,4,8,256]{3,2,1,0:T(8,128)(2,1)} %get-tuple-element.32), channel_id=1, source_target_pairs={{0,1},{1,2},{2,3},{3,0},{4,5},{5,6},{6,7},{7,4},{8,9},{9,10},{10,1... | collective-permute-start | bytes 442376 | tf_op jit(solution)/shard_map/ppermute | solution.py:22
  10.9 5.5 %collective-permute-start.1 = (bf16[9,4,8,256]{3,2,1,0:T(8,128)(2,1)}, bf16[9,4,8,256]{3,2,1,0:T(8,128)(2,1)S(1)}, u32[]{:S(2)}, u32[]{:S(2)}) collective-permute-start(bf16[9,4,8,256]{3,2,1,0:T(8,128)(2,1)} %get-tuple-element.33), channel_id=1, source_target_pairs={{0,3},{1,0},{2,1},{3,2},{4,7},{5,4},{6,5},{7,6},{8,11},{9,8},{10,9... | collective-permute-start | bytes 442376 | tf_op jit(solution)/shard_map/ppermute | solution.py:22
  17.4 0.7 copy-start.1
  18.0 30.9 %collective-permute-start.3 = (bf16[9,1,128,256]{3,2,1,0:T(8,128)(2,1)}, bf16[9,1,128,256]{3,2,1,0:T(8,128)(2,1)}, u32[]{:S(2)}, u32[]{:S(2)}) collective-permute-start(bf16[9,1,128,256]{3,2,1,0:T(8,128)(2,1)} %get-tuple-element.38), channel_id=1, source_target_pairs={{0,4},{4,8},{8,12},{12,16},{16,20},{20,24},{24,28},{28,0},{1,5},{5... | collective-permute-start | bytes 1769480 | tf_op jit(solution)/shard_map/ppermute | solution.py:22
  20.9 11.1 %collective-permute-start.6 = (bf16[256,768]{1,0:T(8,128)(2,1)S(1)}, bf16[256,768]{1,0:T(8,128)(2,1)}, u32[]{:S(2)}, u32[]{:S(2)}) collective-permute-start(bf16[256,768]{1,0:T(8,128)(2,1)S(1)} %bitcast.4), channel_id=1, source_target_pairs={{0,2},{1,3},{2,0},{3,1},{4,6},{5,7},{6,4},{7,5},{8,10},{9,11},{10,... | collective-permute-start | bytes 1179656 | tf_op jit(solution)/shard_map/ppermute | solution.py:26
  22.4 47.0 %collective-permute-start.2 = (bf16[9,1,128,256]{3,2,1,0:T(8,128)(2,1)S(1)}, bf16[9,1,128,256]{3,2,1,0:T(8,128)(2,1)}, u32[]{:S(2)}, u32[]{:S(2)}) collective-permute-start(bf16[9,1,128,256]{3,2,1,0:T(8,128)(2,1)S(1)} %get-tuple-element.34), channel_id=1, source_target_pairs={{0,28},{4,0},{8,4},{12,8},{16,12},{20,16},{24,20},{28,24},{1,29},{... | collective-permute-start | bytes 1769480 | tf_op jit(solution)/shard_map/ppermute | solution.py:22
  24.8 30.5 %collective-permute-start.5 = (bf16[256,768]{1,0:T(8,128)(2,1)S(1)}, bf16[256,768]{1,0:T(8,128)(2,1)}, u32[]{:S(2)}, u32[]{:S(2)}) collective-permute-start(bf16[256,768]{1,0:T(8,128)(2,1)S(1)} %bitcast.5), channel_id=1, source_target_pairs={{0,1},{1,0},{2,3},{3,2},{4,5},{5,4},{6,7},{7,6},{8,9},{9,8},{10,11... | collective-permute-start | bytes 1179656 | tf_op jit(solution)/shard_map/ppermute | solution.py:26
  24.8 28.7 %all-to-all-start.1 = ((bf16[8,8,2304]{2,1,0:T(8,128)(2,1)}), bf16[8,8,2304]{2,1,0:T(8,128)(2,1)S(1)}, u32[]{:S(2)}, u32[]{:S(2)}) async-start(bf16[8,8,2304]{2,1,0:T(8,128)(2,1)} %get-tuple-element.41), calls=%async_computation.1 | async-start | bytes 589824 | tf_op jit(solution)/shard_map/all_to_all | solution.py:516
  32.0 23.2 %collective-permute-start.7 = (bf16[256,768]{1,0:T(8,128)(2,1)}, bf16[256,768]{1,0:T(8,128)(2,1)}, u32[]{:S(2)}, u32[]{:S(2)}) collective-permute-start(bf16[256,768]{1,0:T(8,128)(2,1)} %collective-permute-done.6.rest_2_), channel_id=1, source_target_pairs={{0,1},{1,0},{2,3},{3,2},{4,5},{5,4},{6,7},{7,6},{8,9},{9,8},{10,11... | collective-permute-start | bytes 1179656 | tf_op jit(solution)/shard_map/ppermute | solution.py:26
  49.0 0.9 %copy-start.2 = (bf16[9,4,8,256]{3,2,1,0:T(8,128)(2,1)S(1)}, bf16[9,4,8,256]{3,2,1,0:T(8,128)(2,1)}, u32[]{:S(2)}) copy-start(bf16[9,4,8,256]{3,2,1,0:T(8,128)(2,1)} %copy-done.1) | copy-start | bytes 442372
  51.9 1.6 %copy-start.6 = (bf16[9,5,128,256]{3,2,1,0:T(8,128)(2,1)}, bf16[9,5,128,256]{3,2,1,0:T(8,128)(2,1)S(1)}, u32[]{:S(2)}) copy-start(bf16[9,5,128,256]{3,2,1,0:T(8,128)(2,1)S(1)} %build.1.x) | copy-start | bytes 8847364
  53.5 15.4 %collective-permute-start.4 = (bf16[8,8,2304]{2,1,0:T(8,128)(2,1)S(1)}, bf16[8,8,2304]{2,1,0:T(8,128)(2,1)S(1)}, u32[]{:S(2)}, u32[]{:S(2)}) collective-permute-start(bf16[8,8,2304]{2,1,0:T(8,128)(2,1)S(1)} %all-to-all-done.1.rest_0_), channel_id=1, source_target_pairs={{0,2},{1,3},{2,0},{3,1},{4,6},{5,7},{6,4},{7,5},{8,10},{9,11},{10,... | collective-permute-start | bytes 884744 | tf_op jit(solution)/shard_map/ppermute | solution.py:26
  55.2 1.8 %copy-start.7 = (bf16[9,5,128,256]{3,2,1,0:T(8,128)(2,1)S(1)}, bf16[9,5,128,256]{3,2,1,0:T(8,128)(2,1)}, u32[]{:S(2)}) copy-start(bf16[9,5,128,256]{3,2,1,0:T(8,128)(2,1)} %copy-done.6) | copy-start | bytes 8847364
  63.7 19.2 %collective-permute-start.8 = (bf16[9,128,256]{2,1,0:T(8,128)(2,1)S(1)}, bf16[9,128,256]{2,1,0:T(8,128)(2,1)S(1)}, u32[]{:S(2)}, u32[]{:S(2)}) collective-permute-start(bf16[9,128,256]{2,1,0:T(8,128)(2,1)S(1)} %get-tuple-element.49), channel_id=1, source_target_pairs={{0,28},{4,0},{8,4},{12,8},{16,12},{20,16},{24,20},{28,24},{1,29},{... | collective-permute-start | bytes 1769480 | tf_op jit(solution)/shard_map/ppermute | solution.py:22
  68.9 4.8 %collective-permute-start.9 = (bf16[8,8,2304]{2,1,0:T(8,128)(2,1)S(1)}, bf16[8,8,2304]{2,1,0:T(8,128)(2,1)S(1)}, u32[]{:S(2)}, u32[]{:S(2)}) collective-permute-start(bf16[8,8,2304]{2,1,0:T(8,128)(2,1)S(1)} %all-to-all-done.1.rest_0_), channel_id=1, source_target_pairs={{0,1},{1,0},{2,3},{3,2},{4,5},{5,4},{6,7},{7,6},{8,9},{9,8},{10,11... | collective-permute-start | bytes 884744 | tf_op jit(solution)/shard_map/ppermute | solution.py:26
  68.9 4.9 %collective-permute-start.10 = (bf16[8,8,2304]{2,1,0:T(8,128)(2,1)S(1)}, bf16[8,8,2304]{2,1,0:T(8,128)(2,1)S(1)}, u32[]{:S(2)}, u32[]{:S(2)}) collective-permute-start(bf16[8,8,2304]{2,1,0:T(8,128)(2,1)S(1)} %collective-permute-done.4.rest_2_), channel_id=1, source_target_pairs={{0,1},{1,0},{2,3},{3,2},{4,5},{5,4},{6,7},{7,6},{8,9},{9,8},{10,11... | collective-permute-start | bytes 884744 | tf_op jit(solution)/shard_map/ppermute | solution.py:26
  69.4 13.5 %copy-start.3 = (f32[256]{0:T(256)S(1)}, f32[256]{0:T(256)}, u32[]{:S(2)}) copy-start(f32[256]{0:T(256)} %param.11) | copy-start | bytes 3076
  69.4 13.5 %copy-start.4 = (f32[256]{0:T(256)S(1)}, f32[256]{0:T(256)}, u32[]{:S(2)}) copy-start(f32[256]{0:T(256)} %param.12) | copy-start | bytes 3076
  69.4 13.5 %copy-start.5 = (f32[256]{0:T(256)S(1)}, f32[256]{0:T(256)}, u32[]{:S(2)}) copy-start(f32[256]{0:T(256)} %param.13) | copy-start | bytes 3076

commit v3 on v2

--- a/solution.py
+++ b/solution.py
@@ -52,74 +52,61 @@
     )(*sources)
 
 
-def side_columns(frames):
+def side_columns(frames, weights=(), copies=0, part=0):
     n_frames, rows, cols, channels = frames.shape
+    width = 3 * channels
     side = jax.ShapeDtypeStruct((n_frames, rows, SIDE, channels), frames.dtype)
-
-    def body(source, first, last, first_kept, last_kept, sems, out_sems):
-        moves = [
-            (source.at[:, :, 0:SIDE], first_kept, first),
-            (source.at[:, :, cols - SIDE :], last_kept, last),
+    kept, picks = [side, side], []
+    if weights:
+        spatial, temporal, down = weights
+        kept += [
+            jax.ShapeDtypeStruct((spatial.shape[0], width), spatial.dtype),
+            jax.ShapeDtypeStruct((part, down.shape[1]), down.dtype),
         ]
+        picks = [
+            (n, at)
+            for n, w in enumerate((spatial, temporal))
+            for at in range(0, w.shape[1], width)
+        ]
+    count = len(kept)
+    outs = kept[:2] + [
+        jax.ShapeDtypeStruct((copies,) + k.shape, k.dtype) for k in kept[2:]
+    ]
+
+    def body(source, *refs):
+        taps, refs = refs[: len(weights)], refs[len(weights) :]
+        targets, holds, (sems, out_sems) = refs[:count], refs[count:-2], refs[-2:]
+        slices = [source.at[:, :, 0:SIDE], source.at[:, :, cols - SIDE :]]
+        if weights:
+            chan = lax.axis_index("chan")
+            start = pl.multiple_of(chan * part, part)
+            slices += [taps[0].at[:, 0:width], taps[2].at[pl.ds(start, part)]]
+            for k, (n, at) in enumerate(picks):
+                @pl.when(chan == k)
+                def _():
+                    pltpu.make_async_copy(
+                        taps[n].at[:, at : at + width], holds[2], sems.at[2]
+                    ).start()
         fetches = [
             pltpu.make_async_copy(src, hold, sems.at[k])
-            for k, (src, hold, _) in enumerate(moves)
+            for k, (src, hold) in enumerate(zip(slices, holds))
         ]
-        stores = [
-            pltpu.make_async_copy(hold, dst, out_sems.at[k])
-            for k, (_, hold, dst) in enumerate(moves)
-        ]
-        for fetch in fetches:
-            fetch.start()
-        for fetch, store in zip(fetches, stores):
-            fetch.wait()
-            store.start()
-        for store in stores:
-            store.wait()
-
-    return staged_call(body, [frames], [side, side], [side, side], (2, 2), "side_columns")
-
-
-def weight_pieces(spatial, temporal, down, channels, copies, part):
-    width = 3 * channels
-    depth = spatial.shape[0]
-    tap = jax.ShapeDtypeStruct((depth, width), spatial.dtype)
-    own = jax.ShapeDtypeStruct((part, down.shape[1]), down.dtype)
-    picks = [
-        (n, at) for n, w in enumerate((spatial, temporal)) for at in range(0, w.shape[1], width)
-    ]
-
-    def body(*refs):
-        taps, down_ref = refs[:2], refs[2]
-        outs, kept, (sems, out_sems) = refs[3:5], refs[5:7], refs[7:]
-        chan = lax.axis_index("chan")
-        for k, (n, at) in enumerate(picks):
-            @pl.when(chan == k)
-            def _():
-                pltpu.make_async_copy(
-                    taps[n].at[:, at : at + width], kept[0], sems.at[0]
-                ).start()
-        rows = down_ref.at[pl.ds(pl.multiple_of(chan * part, part), part)]
-        fetches = [
-            pltpu.make_async_copy(taps[0].at[:, 0:width], kept[0], sems.at[0]),
-            pltpu.make_async_copy(rows, kept[1], sems.at[1]),
-        ]
-        fetches[1].start()
+        for k, fetch in enumerate(fetches):
+            if k != 2:
+                fetch.start()
         stores = []
         for k, fetch in enumerate(fetches):
             fetch.wait()
-            for j in range(copies):
-                store = pltpu.make_async_copy(
-                    kept[k], outs[k].at[j], out_sems.at[len(stores)]
-                )
+            for target in [targets[k]] if k < 2 else [targets[k].at[j] for j in range(copies)]:
+                store = pltpu.make_async_copy(holds[k], target, out_sems.at[len(stores)])
                 store.start()
                 stores.append(store)
         for store in stores:
             store.wait()
 
-    outs = [jax.ShapeDtypeStruct((copies,) + k.shape, k.dtype) for k in (tap, own)]
+    moves = 2 + (count - 2) * copies
     return staged_call(
-        body, [spatial, temporal, down], [tap, own], outs, (2, 2 * copies), "weight_pieces"
+        body, [frames, *weights], kept, outs, (count, moves), "side_columns"
     )
 
 
@@ -141,7 +128,7 @@
     n_frames, rows, cols, channels = frames.shape
     row = (n_frames, 1, cols, channels)
     full = (n_frames, 1, LANE_COLS, channels)
-    wide = jax.ShapeDtypeStruct(full, BF16)
+    wide = pltpu.HBM(full, BF16)
     return pl.pallas_call(
         extended_kernel,
         grid=(1,),
@@ -178,53 +165,53 @@
     )
 
 
-def build_kernel(frames, pack, top, x):
+def build_kernel(frames, pack, x):
     cols = frames.shape[2]
-    rows = frames.shape[1]
+    x[:, :, :cols] = frames[...]
+    x[:, :, cols:] = pack[...]
+
+
+def build_call(frames, pack):
+    n_frames, rows, cols, channels = frames.shape
+    return pl.pallas_call(
+        build_kernel,
+        in_specs=in_vmem(2),
+        out_specs=pl.BlockSpec(memory_space=pltpu.VMEM),
+        out_shape=pltpu.VMEM((n_frames, rows, LANE_COLS, channels), BF16),
+        compiler_params=params(8, grid=0),
+        cost_estimate=cost(0, 5),
+        name="build",
+    )(frames, pack)
+
+
+def masked_kernel(top, kept):
     outside = lax.axis_index("rows") == 0
-    zero = jnp.zeros((), BF16)
-    x[:, 0:1] = jnp.where(outside, zero, top[...])
-    x[:, 1 : rows + 1, :cols] = frames[...]
-    x[:, 1 : rows + 1, cols:] = pack[...]
-
-
-def build_call(frames, pack, top):
-    n_frames, rows, cols, channels = frames.shape
-    batch = 3 if n_frames % 3 == 0 else 1
-    shape = (n_frames, rows + 1, LANE_COLS, channels)
-    return pl.pallas_call(
-        build_kernel,
-        grid=(n_frames // batch,),
-        in_specs=[
-            by_frame(rows, cols, channels, batch=batch),
-            by_frame(rows, SIDE, channels, batch=batch),
-            by_frame(1, LANE_COLS, channels, batch=batch),
-        ],
-        out_specs=by_frame(*shape[1:], batch=batch),
-        out_shape=jax.ShapeDtypeStruct(shape, BF16),
-        compiler_params=params(16),
+    kept[...] = jnp.where(outside, jnp.zeros((), BF16), top[...])
+
+
+def masked_call(top):
+    return pl.pallas_call(
+        masked_kernel,
+        in_specs=in_vmem(1),
+        out_specs=pl.BlockSpec(memory_space=pltpu.VMEM),
+        out_shape=pltpu.VMEM(top.shape, BF16),
+        compiler_params=params(4, grid=0),
         cost_estimate=cost(30 << 30, 64),
-        name="build",
-    )(frames, pack, top)
-
-
-def inner_kernel(x, *rest, split):
+        name="masked",
+    )(top)
+
+
+def inner_kernel(x, top, *rest, split):
     part_refs = rest[:4]
     first_row, middle, border, weight = rest[4:]
     n_frames, rows, _, channels = x.shape
-    rows = rows - 1
     chan = lax.axis_index("chan") if split else 0
     for k, part in enumerate(part_refs):
         weight[chan ^ k] = part[...]
 
-    def conv(f, many, row, count, taps):
-        lhs = jnp.concatenate(
-            [
-                x[pl.ds(f, many), row + a : row + a + count].reshape(-1, channels)
-                for a in range(taps)
-            ],
-            axis=1,
-        )
+    def conv(lhs):
+        taps = len(lhs)
+        lhs = jnp.concatenate([block.reshape(-1, channels) for block in lhs], axis=1)
         kernel = weight[:taps].reshape(taps * channels, 3 * channels)
         return side_shift(jnp.dot(lhs, kernel, preferred_element_type=F32))
 
@@ -232,11 +219,17 @@
 
     def frames(g, _):
         at = pl.ds(g * many, many)
-        first = conv(g * many, many, 0, rows - 1, 3).astype(BF16)
+        first = conv(
+            [
+                jnp.concatenate([top[at], x[at, : rows - 2]], axis=1),
+                x[at, : rows - 1],
+                x[at, 1:],
+            ]
+        ).astype(BF16)
         first = first.reshape(many, rows - 1, LANE_COLS, channels)
         first_row[at] = first[:, 0]
         middle[at] = first.reshape(many, -1, channels)
-        border[at] = conv(g * many, many, rows - 1, 1, 2)
+        border[at] = conv([x[at, rows - 2], x[at, rows - 1]])
         return 0
 
     lax.fori_loop(0, n_frames // many, frames, 0, unroll=True)
@@ -425,13 +418,11 @@
     return [pl.BlockSpec(memory_space=pltpu.VMEM)] * count
 
 
-def inner_call(x, front_parts, split):
+def inner_call(x, top, front_parts, split):
     n_frames, rows, _, channels = x.shape
-    rows = rows - 1
-    tap = 2 * n_frames * LANE_COLS * channels * channels
     return pl.pallas_call(
         functools.partial(inner_kernel, split=split),
-        in_specs=in_vmem(5),
+        in_specs=in_vmem(6),
         out_specs=in_vmem(4),
         out_shape=[
             jax.ShapeDtypeStruct((n_frames, LANE_COLS, channels), BF16),
@@ -440,9 +431,9 @@
             jax.ShapeDtypeStruct((4, channels, 3 * channels), BF16),
         ],
         compiler_params=params(24, grid=0),
-        cost_estimate=cost(33 * tap, 8),
+        cost_estimate=cost(5 << 30, 8),
         name="inner",
-    )(x, *front_parts)
+    )(x, top, *front_parts)
 
 
 def outer_call(bottom, middle, border, weight, cols, devices):
@@ -498,20 +489,25 @@
     row_devices, chan_devices = lax.axis_size("rows"), lax.axis_size("chan")
     part = spatial_weight.shape[0] // chan_devices
     split = part % 8 == 0 and chan_devices == 4
-    first_cols, last_cols = side_columns(frames)
+    if split:
+        first_cols, last_cols, taps, own = side_columns(
+            frames, (spatial_weight, temporal_weight, down_weight), row_devices, part
+        )
+    else:
+        first_cols, last_cols = side_columns(frames)
     right = shifted(first_cols, "chan", -1)
     left = shifted(last_cols, "chan", 1)
     low_row, high_row, pack = extended_call(frames, left, right)
     top = shifted(low_row, "rows", 1)
 
     if split:
-        taps, own = weight_pieces(
-            spatial_weight, temporal_weight, down_weight, channels, row_devices, part
-        )
         taps = lax.all_to_all(taps, "rows", 0, 0)
-        taps, pack = lax.optimization_barrier((taps, pack))
+        taps, _ = lax.optimization_barrier((taps, pack))
+        taps = taps.reshape(channels, 3 * channels)
+        over = swapped(taps, "chan", 2)
+        over, high_row = lax.optimization_barrier((over, high_row))
         bottom = shifted(high_row, "rows", -1)
-        front_parts = spread_chan(taps.reshape(channels, 3 * channels))
+        front_parts = [taps, swapped(taps, "chan", 1), over, swapped(over, "chan", 1)]
         own, taps = lax.optimization_barrier((own, taps))
         own = lax.all_to_all(own, "rows", 0, 0)
     else:
@@ -522,13 +518,14 @@
         front_parts = [taps[:, k * width : (k + 1) * width] for k in range(4)]
         own = lax.all_gather(down_weight, "rows", axis=0, tiled=True)
 
-    x = build_call(frames, pack, top)
-    x, own = lax.optimization_barrier((x, own))
+    x = build_call(frames, pack)
+    own, top = lax.optimization_barrier((own, top))
+    top = masked_call(top)
     across = swapped(own, "chan", 2) if split else own
-    first_row, middle, border, weight = inner_call(x, front_parts, split)
+    first_row, middle, border, weight = inner_call(x, top, front_parts, split)
     halo = shifted(first_row, "rows", -1)
     if split:
-        own, across, middle = lax.optimization_barrier((own, across, middle))
+        own, across, _ = lax.optimization_barrier((own, across, middle))
         back_parts = [own, swapped(own, "chan", 1), across, swapped(across, "chan", 1)]
     else:
         back_parts = [own.reshape(channels // 8, 8, -1)]

time: 87.7 us -> 74.1 us (0.84)
  waiting for transfers between devices: 25.4 us -> 14.1 us
  local copies, waits for them, and re-layouts: 6.37 us -> 2.82 us
  blocking collectives: 9.12 us -> 11.4 us
  Pallas kernels: 20.3 us -> 18.5 us
  starting transfers between devices: 25.8 us -> 26.7 us
    ppermute x5, waiting for transfers between devices: 20.7 us -> 3.76 us  [shifted(): lax.ppermute(block, axis, [(i, (i + distance) % count) for i in range(cou...]
    unnamed x16 -> x12, local copies, waits for them, and re-layouts: 5 us -> 1.45 us
    ppermute x6, waiting for transfers between devices: 3.83 us -> 7.32 us  [swapped(): lax.ppermute(block, axis, [(i, i ^ bit) for i in range(lax.axis_size(axis...]
    all_to_all x1, blocking collectives: 9.12 us -> 11.4 us  [per_device(): all_stats = lax.all_to_all(stats, ('rows', 'chan'), 0, 0)]
    all_to_all x1, waiting for transfers between devices: 0.83 us -> 3.06 us  [per_device(): taps = lax.all_to_all(taps, 'rows', 0, 0)]
    pallas_call x2 -> x1, Pallas kernels: 3.59 us -> 2.22 us  [staged_call(): pl.pallas_call(body, out_shape=outs, in_specs=[pl.BlockSpec(memory_space=...]
    pallas_call x1 -> x2, Pallas kernels: 2.02 us -> 1.26 us  [the longest x1 1.1 us: masked_call(): pl.pallas_call(masked_kernel, in_specs=in_vmem(1), out_specs=pl.BlockSpec...]
  transfers between devices with their start and end apart: 13 -> 13, of which waited for: 5 -> 4; matrix products, arithmetic and copies ran while one was open for 0% -> 0% of each run, Pallas kernels for 18% -> 18%
where the time goes in v3:
time: 74.1 us; the launch traced here: 73.7 us
  starting transfers between devices  26.7 us (36%)
  Pallas kernels  18.5 us (25%)
  waiting for transfers between devices  14.1 us (19%)
  blocking collectives  11.4 us (15%)
  local copies, waits for them, and re-layouts  2.82 us (4%)
    ppermute x5, starting transfers between devices, shifted(): lax.ppermute(block, axis, [(i, (i + distance) % count) for i in range(cou...  12.2 us
    all_to_all x1, blocking collectives, per_device(): all_stats = lax.all_to_all(stats, ('rows', 'chan'), 0, 0)  11.4 us
    ppermute x6, waiting for transfers between devices, swapped(): lax.ppermute(block, axis, [(i, i ^ bit) for i in range(lax.axis_size(axis...  7.32 us
    all_to_all x1, starting transfers between devices, per_device(): taps = lax.all_to_all(taps, 'rows', 0, 0)  7.26 us
    pallas_call x1, Pallas kernels, inner_call(): pl.pallas_call(functools.partial(inner_kernel, split=split), in_specs=in_...  6.46 us
    pallas_call x1, Pallas kernels, outer_call(): pl.pallas_call(functools.partial(outer_kernel, cols=cols), in_specs=in_vm...  4.41 us
    ppermute x5, waiting for transfers between devices, shifted(): lax.ppermute(block, axis, [(i, (i + distance) % count) for i in range(cou...  3.76 us
    all_to_all x1, starting transfers between devices, per_device(): own = lax.all_to_all(own, 'rows', 0, 0)  3.62 us
  transfers between devices with their start and end apart: 13, of which 4 were waited for; matrix products, arithmetic and copies ran while one was open for 0% of the time, Pallas kernels for 18%

profile of v3, /device:TPU:0, one launch (start us, length us, event | category | flops | bytes accessed | tf_op | source)
XLA Modules:
  0.0 73.7 jit_solution(8999559723762802862)
XLA Ops:
  0.0 2.2 %side_columns.1 = (bf16[9,4,8,256]{3,2,1,0:T(8,128)(2,1)}, bf16[9,4,8,256]{3,2,1,0:T(8,128)(2,1)}, bf16[8,32,768]{2,1,0:T(8,128)(2,1)}, bf16[8,8,2304]{2,1,0:T(8,128)(2,1)}) custom-call(bf16[9,4,120,256]{3,2,1,0:T(8,128)(2,1)} %frames.1, bf16[32,2304]{1,0:T(8,128)(2,1)} %refs_0_.1, bf16[32,768]{1,0:T(8,128)(2,1)} %refs_1_.1, bf16[32,2304]{1,0:T(8,128)(2,1)} %refs_2_.1), custom_call_target="tpu_custom_call" | custom-call | tf_op jit(solution)/shard_map/side_columns/pallas_call | solution.py:43
  2.2 7.3 %all-to-all-start = ((bf16[8,32,768]{2,1,0:T(8,128)(2,1)}), bf16[8,32,768]{2,1,0:T(8,128)(2,1)S(1)}, u32[]{:S(2)}, u32[]{:S(2)}) async-start(bf16[8,32,768]{2,1,0:T(8,128)(2,1)} %get-tuple-element.32), calls=%async_computation | async-start | bytes 786432 | tf_op jit(solution)/shard_map/all_to_all | solution.py:504
  9.5 0.0 collective-permute-start
  9.5 1.7 %collective-permute-start.1 = (bf16[9,4,8,256]{3,2,1,0:T(8,128)(2,1)}, bf16[9,4,8,256]{3,2,1,0:T(8,128)(2,1)S(1)}, u32[]{:S(2)}, u32[]{:S(2)}) collective-permute-start(bf16[9,4,8,256]{3,2,1,0:T(8,128)(2,1)} %get-tuple-element.34), channel_id=1, source_target_pairs={{0,3},{1,0},{2,1},{3,2},{4,7},{5,4},{6,5},{7,6},{8,11},{9,8},{10,9... | collective-permute-start | bytes 442376 | tf_op jit(solution)/shard_map/ppermute | solution.py:22
  11.2 3.0 %collective-permute-done.left = bf16[9,4,8,256]{3,2,1,0:T(8,128)(2,1)S(1)} collective-permute-done((bf16[9,4,8,256]{3,2,1,0:T(8,128)(2,1)}, bf16[9,4,8,256]{3,2,1,0:T(8,128)(2,1)S(1)}, u32[]{:S(2)}, u32[]{:S(2)}) %collective-permute-start) | collective-permute-done | bytes 147488 | tf_op jit(solution)/shard_map/ppermute | solution.py:22
  14.3 0.7 collective-permute-done.1.right
  15.0 1.1 %extended.1 = (bf16[9,1,128,256]{3,2,1,0:T(8,128)(2,1)}, bf16[9,1,128,256]{3,2,1,0:T(8,128)(2,1)}, bf16[9,4,8,256]{3,2,1,0:T(8,128)(2,1)S(1)}) custom-call(bf16[9,4,120,256]{3,2,1,0:T(8,128)(2,1)S(1)} %copy-done, bf16[9,4,120,256]{3,2,1,0:T(8,128)(2,1)S(1)} %copy-done, bf16[9,4,8,256]{3,2,1,0:T(8,128)(2,1)S(1)} %collective-permute-done.left, ...), custom_call_target="tpu_custom_call" | custom-call | bytes 3145728 | tf_op jit(solution)/shard_map/extended/pallas_call | solution.py:132
  16.1 2.0 %collective-permute-start.4 = (bf16[9,1,128,256]{3,2,1,0:T(8,128)(2,1)}, bf16[9,1,128,256]{3,2,1,0:T(8,128)(2,1)}, u32[]{:S(2)}, u32[]{:S(2)}) collective-permute-start(bf16[9,1,128,256]{3,2,1,0:T(8,128)(2,1)} %get-tuple-element.41), channel_id=1, source_target_pairs={{0,4},{4,8},{8,12},{12,16},{16,20},{20,24},{24,28},{28,0},{1,5},{5... | collective-permute-start | bytes 1769480 | tf_op jit(solution)/shard_map/ppermute | solution.py:22
  18.1 3.1 %all-to-all-done = bf16[8,32,768]{2,1,0:T(8,128)(2,1)S(1)} async-done(((bf16[8,32,768]{2,1,0:T(8,128)(2,1)}), bf16[8,32,768]{2,1,0:T(8,128)(2,1)S(1)}, u32[]{:S(2)}, u32[]{:S(2)}) %all-to-all-start) | async-done | bytes 393248 | tf_op jit(solution)/shard_map/all_to_all | solution.py:504
  21.2 3.6 %all-to-all-start.1 = ((bf16[8,8,2304]{2,1,0:T(8,128)(2,1)}), bf16[8,8,2304]{2,1,0:T(8,128)(2,1)S(1)}, u32[]{:S(2)}, u32[]{:S(2)}) async-start(bf16[8,8,2304]{2,1,0:T(8,128)(2,1)} %get-tuple-element.40), calls=%async_computation.1 | async-start | bytes 589824 | tf_op jit(solution)/shard_map/all_to_all | solution.py:512
  24.8 1.5 %collective-permute-start.2 = (bf16[256,768]{1,0:T(8,128)(2,1)S(1)}, bf16[256,768]{1,0:T(8,128)(2,1)S(1)}, u32[]{:S(2)}, u32[]{:S(2)}) collective-permute-start(bf16[256,768]{1,0:T(8,128)(2,1)S(1)} %bitcast.4), channel_id=1, source_target_pairs={{0,2},{1,3},{2,0},{3,1},{4,6},{5,7},{6,4},{7,5},{8,10},{9,11},{10,... | collective-permute-start | bytes 1179656 | tf_op jit(solution)/shard_map/ppermute | solution.py:26
  26.3 0.2 build.1.x
  26.5 1.4 %copy-done.1 = bf16[9,4,128,256]{3,2,1,0:T(8,128)(2,1)} copy-done((bf16[9,4,128,256]{3,2,1,0:T(8,128)(2,1)}, bf16[9,4,128,256]{3,2,1,0:T(8,128)(2,1)S(1)}, u32[]{:S(2)}) %copy-start.1) | copy-done | bytes 2359320
  27.9 7.3 %collective-permute-done.2.rest_2_ = bf16[256,768]{1,0:T(8,128)(2,1)S(1)} collective-permute-done((bf16[256,768]{1,0:T(8,128)(2,1)S(1)}, bf16[256,768]{1,0:T(8,128)(2,1)S(1)}, u32[]{:S(2)}, u32[]{:S(2)}) %collective-permute-start.2) | collective-permute-done | bytes 393248 | tf_op jit(solution)/shard_map/ppermute | solution.py:26
  35.2 4.4 %collective-permute-start.3 = (bf16[9,1,128,256]{3,2,1,0:T(8,128)(2,1)}, bf16[9,1,128,256]{3,2,1,0:T(8,128)(2,1)}, u32[]{:S(2)}, u32[]{:S(2)}) collective-permute-start(bf16[9,1,128,256]{3,2,1,0:T(8,128)(2,1)} %get-tuple-element.38), channel_id=1, source_target_pairs={{0,28},{4,0},{8,4},{12,8},{16,12},{20,16},{24,20},{28,24},{1,29},{... | collective-permute-start | bytes 1769480 | tf_op jit(solution)/shard_map/ppermute | solution.py:22
  39.7 1.1 %masked.1.top = bf16[9,1,128,256]{3,2,1,0:T(8,128)(2,1)S(1)} custom-call(bf16[9,1,128,256]{3,2,1,0:T(8,128)(2,1)} %collective-permute-done.4.top), custom_call_target="tpu_custom_call" | custom-call | flops 32212254720 | bytes 67108864 | tf_op jit(solution)/shard_map/masked/pallas_call | solution.py:193
  40.8 1.6 %collective-permute-start.8 = (bf16[8,8,2304]{2,1,0:T(8,128)(2,1)S(1)}, bf16[8,8,2304]{2,1,0:T(8,128)(2,1)S(1)}, u32[]{:S(2)}, u32[]{:S(2)}) collective-permute-start(bf16[8,8,2304]{2,1,0:T(8,128)(2,1)S(1)} %all-to-all-done.1.rest_0_), channel_id=1, source_target_pairs={{0,2},{1,3},{2,0},{3,1},{4,6},{5,7},{6,4},{7,5},{8,10},{9,11},{10,... | collective-permute-start | bytes 884744 | tf_op jit(solution)/shard_map/ppermute | solution.py:26
  42.4 6.5 %inner.1 = (bf16[9,128,256]{2,1,0:T(8,128)(2,1)S(1)}, bf16[9,384,256]{2,1,0:T(8,128)(2,1)S(1)}, f32[9,128,256]{2,1,0:T(8,128)S(1)}, bf16[4,256,768]{2,1,0:T(8,128)(2,1)S(1)}) custom-call(bf16[9,4,128,256]{3,2,1,0:T(8,128)(2,1)S(1)} %copy-done.2, bf16[9,1,128,256]{3,2,1,0:T(8,128)(2,1)S(1)} %masked.1.top, bf16[256,768]{1,0:T(8,128)(2,1)S(1)} %bitcast.6, ...), custom_call_target="tpu_custom_call" | custom-call | flops 5368709120 | bytes 8388608 | tf_op jit(solution)/shard_map/inner/pallas_call | solution.py:423
  48.9 4.0 %collective-permute-start.7 = (bf16[9,128,256]{2,1,0:T(8,128)(2,1)S(1)}, bf16[9,128,256]{2,1,0:T(8,128)(2,1)S(1)}, u32[]{:S(2)}, u32[]{:S(2)}) collective-permute-start(bf16[9,128,256]{2,1,0:T(8,128)(2,1)S(1)} %get-tuple-element.48), channel_id=1, source_target_pairs={{0,28},{4,0},{8,4},{12,8},{16,12},{20,16},{24,20},{28,24},{1,29},{... | collective-permute-start | bytes 1769480 | tf_op jit(solution)/shard_map/ppermute | solution.py:22
  52.9 0.5 collective-permute-start.10
  53.4 4.4 %outer.1 = (f32[9,4,2,128,128]{4,3,2,1,0:T(8,128)S(1)}, f32[32,2,256]{2,1,0:T(2,128)S(1)}, bf16[768,256]{1,0:T(8,128)(2,1)S(1)}) custom-call(bf16[9,1,128,256]{3,2,1,0:T(8,128)(2,1)} %collective-permute-done.3.bottom, bf16[9,384,256]{2,1,0:T(8,128)(2,1)S(1)} %get-tuple-element.44.middle, f32[9,128,256]{2,1,0:T(8,128)S(1)} %get-tuple-element.45.border, ...), custom_call_target="tpu_custom_call" | custom-call | flops 2264924160 | bytes 10485760 | tf_op jit(solution)/shard_map/outer/pallas_call | solution.py:443
  57.8 11.4 %all_to_all.15.stats = f32[32,2,256]{2,1,0:T(2,128)S(1)} all-to-all(f32[32,2,256]{2,1,0:T(2,128)S(1)} %get-tuple-element.54), channel_id=1, replica_groups=mesh['rows'=8,'chan'=4] {'rows','chan'}, dimensions={0} | all-to-all | bytes 131072 | tf_op jit(solution)/shard_map/all_to_all | solution.py:536
  69.3 3.0 %back.1 = bf16[9,2,60,256]{3,2,1,0:T(8,128)(2,1)S(1)} custom-call(f32[9,4,2,128,128]{4,3,2,1,0:T(8,128)S(1)} %get-tuple-element.47.hidden, bf16[9,128,256]{2,1,0:T(8,128)(2,1)S(1)} %collective-permute-done.7.halo, bf16[768,256]{1,0:T(8,128)(2,1)S(1)} %get-tuple-element.49.temporal, f32[32,2,256]{2,1,0:T(2,128)S(1)} %all_to_all.15.stats, ...), custom_call_target="tpu_custom_call" | custom-call | flops 1811939328 | bytes 10485760 | tf_op jit(solution)/shard_map/back/pallas_call | solution.py:467
  72.3 1.4 %copy.8 = bf16[9,2,60,256]{3,1,2,0:T(2,128)(2,1)} copy(bf16[9,2,60,256]{3,2,1,0:T(8,128)(2,1)S(1)} %back.1) | data formatting | bytes 1105920 | tf_op jit(solution)/shard_map/back/pallas_call | solution.py:467
  (23 shorter events, 0.1 us)
Async XLA Ops:
  0.0 15.0 %copy-start = (bf16[9,4,120,256]{3,2,1,0:T(8,128)(2,1)S(1)}, bf16[9,4,120,256]{3,2,1,0:T(8,128)(2,1)}, u32[]{:S(2)}) copy-start(bf16[9,4,120,256]{3,2,1,0:T(8,128)(2,1)} %frames.1) | copy-start | bytes 6635524
  2.2 19.0 %all-to-all-start = ((bf16[8,32,768]{2,1,0:T(8,128)(2,1)}), bf16[8,32,768]{2,1,0:T(8,128)(2,1)S(1)}, u32[]{:S(2)}, u32[]{:S(2)}) async-start(bf16[8,32,768]{2,1,0:T(8,128)(2,1)} %get-tuple-element.32), calls=%async_computation | async-start | bytes 786432 | tf_op jit(solution)/shard_map/all_to_all | solution.py:504
  9.5 4.8 %collective-permute-start = (bf16[9,4,8,256]{3,2,1,0:T(8,128)(2,1)}, bf16[9,4,8,256]{3,2,1,0:T(8,128)(2,1)S(1)}, u32[]{:S(2)}, u32[]{:S(2)}) collective-permute-start(bf16[9,4,8,256]{3,2,1,0:T(8,128)(2,1)} %get-tuple-element.33), channel_id=1, source_target_pairs={{0,1},{1,2},{2,3},{3,0},{4,5},{5,6},{6,7},{7,4},{8,9},{9,10},{10,1... | collective-permute-start | bytes 442376 | tf_op jit(solution)/shard_map/ppermute | solution.py:22
  9.5 5.5 %collective-permute-start.1 = (bf16[9,4,8,256]{3,2,1,0:T(8,128)(2,1)}, bf16[9,4,8,256]{3,2,1,0:T(8,128)(2,1)S(1)}, u32[]{:S(2)}, u32[]{:S(2)}) collective-permute-start(bf16[9,4,8,256]{3,2,1,0:T(8,128)(2,1)} %get-tuple-element.34), channel_id=1, source_target_pairs={{0,3},{1,0},{2,1},{3,2},{4,7},{5,4},{6,5},{7,6},{8,11},{9,8},{10,9... | collective-permute-start | bytes 442376 | tf_op jit(solution)/shard_map/ppermute | solution.py:22
  16.1 23.6 %collective-permute-start.4 = (bf16[9,1,128,256]{3,2,1,0:T(8,128)(2,1)}, bf16[9,1,128,256]{3,2,1,0:T(8,128)(2,1)}, u32[]{:S(2)}, u32[]{:S(2)}) collective-permute-start(bf16[9,1,128,256]{3,2,1,0:T(8,128)(2,1)} %get-tuple-element.41), channel_id=1, source_target_pairs={{0,4},{4,8},{8,12},{12,16},{16,20},{20,24},{24,28},{28,0},{1,5},{5... | collective-permute-start | bytes 1769480 | tf_op jit(solution)/shard_map/ppermute | solution.py:22
  21.2 18.5 %all-to-all-start.1 = ((bf16[8,8,2304]{2,1,0:T(8,128)(2,1)}), bf16[8,8,2304]{2,1,0:T(8,128)(2,1)S(1)}, u32[]{:S(2)}, u32[]{:S(2)}) async-start(bf16[8,8,2304]{2,1,0:T(8,128)(2,1)} %get-tuple-element.40), calls=%async_computation.1 | async-start | bytes 589824 | tf_op jit(solution)/shard_map/all_to_all | solution.py:512
  24.8 10.4 %collective-permute-start.2 = (bf16[256,768]{1,0:T(8,128)(2,1)S(1)}, bf16[256,768]{1,0:T(8,128)(2,1)S(1)}, u32[]{:S(2)}, u32[]{:S(2)}) collective-permute-start(bf16[256,768]{1,0:T(8,128)(2,1)S(1)} %bitcast.4), channel_id=1, source_target_pairs={{0,2},{1,3},{2,0},{3,1},{4,6},{5,7},{6,4},{7,5},{8,10},{9,11},{10,... | collective-permute-start | bytes 1179656 | tf_op jit(solution)/shard_map/ppermute | solution.py:26
  26.5 1.4 %copy-start.1 = (bf16[9,4,128,256]{3,2,1,0:T(8,128)(2,1)}, bf16[9,4,128,256]{3,2,1,0:T(8,128)(2,1)S(1)}, u32[]{:S(2)}) copy-start(bf16[9,4,128,256]{3,2,1,0:T(8,128)(2,1)S(1)} %build.1.x) | copy-start | bytes 7077892
  27.9 14.5 %collective-permute-start.5 = (bf16[256,768]{1,0:T(8,128)(2,1)S(1)}, bf16[256,768]{1,0:T(8,128)(2,1)}, u32[]{:S(2)}, u32[]{:S(2)}) collective-permute-start(bf16[256,768]{1,0:T(8,128)(2,1)S(1)} %bitcast.5), channel_id=1, source_target_pairs={{0,1},{1,0},{2,3},{3,2},{4,5},{5,4},{6,7},{7,6},{8,9},{9,8},{10,11... | collective-permute-start | bytes 1179656 | tf_op jit(solution)/shard_map/ppermute | solution.py:26
  35.2 7.2 %copy-start.2 = (bf16[9,4,128,256]{3,2,1,0:T(8,128)(2,1)S(1)}, bf16[9,4,128,256]{3,2,1,0:T(8,128)(2,1)}, u32[]{:S(2)}) copy-start(bf16[9,4,128,256]{3,2,1,0:T(8,128)(2,1)} %copy-done.1) | copy-start | bytes 7077892
  35.2 18.1 %collective-permute-start.3 = (bf16[9,1,128,256]{3,2,1,0:T(8,128)(2,1)}, bf16[9,1,128,256]{3,2,1,0:T(8,128)(2,1)}, u32[]{:S(2)}, u32[]{:S(2)}) collective-permute-start(bf16[9,1,128,256]{3,2,1,0:T(8,128)(2,1)} %get-tuple-element.38), channel_id=1, source_target_pairs={{0,28},{4,0},{8,4},{12,8},{16,12},{20,16},{24,20},{28,24},{1,29},{... | collective-permute-start | bytes 1769480 | tf_op jit(solution)/shard_map/ppermute | solution.py:22
  39.7 2.7 %collective-permute-start.6 = (bf16[256,768]{1,0:T(8,128)(2,1)S(1)}, bf16[256,768]{1,0:T(8,128)(2,1)}, u32[]{:S(2)}, u32[]{:S(2)}) collective-permute-start(bf16[256,768]{1,0:T(8,128)(2,1)S(1)} %collective-permute-done.2.rest_2_), channel_id=1, source_target_pairs={{0,1},{1,0},{2,3},{3,2},{4,5},{5,4},{6,7},{7,6},{8,9},{9,8},{10,11... | collective-permute-start | bytes 1179656 | tf_op jit(solution)/shard_map/ppermute | solution.py:26
  40.8 12.1 %collective-permute-start.8 = (bf16[8,8,2304]{2,1,0:T(8,128)(2,1)S(1)}, bf16[8,8,2304]{2,1,0:T(8,128)(2,1)S(1)}, u32[]{:S(2)}, u32[]{:S(2)}) collective-permute-start(bf16[8,8,2304]{2,1,0:T(8,128)(2,1)S(1)} %all-to-all-done.1.rest_0_), channel_id=1, source_target_pairs={{0,2},{1,3},{2,0},{3,1},{4,6},{5,7},{6,4},{7,5},{8,10},{9,11},{10,... | collective-permute-start | bytes 884744 | tf_op jit(solution)/shard_map/ppermute | solution.py:26
  48.9 20.4 %collective-permute-start.7 = (bf16[9,128,256]{2,1,0:T(8,128)(2,1)S(1)}, bf16[9,128,256]{2,1,0:T(8,128)(2,1)S(1)}, u32[]{:S(2)}, u32[]{:S(2)}) collective-permute-start(bf16[9,128,256]{2,1,0:T(8,128)(2,1)S(1)} %get-tuple-element.48), channel_id=1, source_target_pairs={{0,28},{4,0},{8,4},{12,8},{16,12},{20,16},{24,20},{28,24},{1,29},{... | collective-permute-start | bytes 1769480 | tf_op jit(solution)/shard_map/ppermute | solution.py:22
  52.9 4.9 %collective-permute-start.9 = (bf16[8,8,2304]{2,1,0:T(8,128)(2,1)S(1)}, bf16[8,8,2304]{2,1,0:T(8,128)(2,1)S(1)}, u32[]{:S(2)}, u32[]{:S(2)}) collective-permute-start(bf16[8,8,2304]{2,1,0:T(8,128)(2,1)S(1)} %all-to-all-done.1.rest_0_), channel_id=1, source_target_pairs={{0,1},{1,0},{2,3},{3,2},{4,5},{5,4},{6,7},{7,6},{8,9},{9,8},{10,11... | collective-permute-start | bytes 884744 | tf_op jit(solution)/shard_map/ppermute | solution.py:26
  52.9 5.0 %collective-permute-start.10 = (bf16[8,8,2304]{2,1,0:T(8,128)(2,1)S(1)}, bf16[8,8,2304]{2,1,0:T(8,128)(2,1)S(1)}, u32[]{:S(2)}, u32[]{:S(2)}) collective-permute-start(bf16[8,8,2304]{2,1,0:T(8,128)(2,1)S(1)} %collective-permute-done.8.rest_2_), channel_id=1, source_target_pairs={{0,1},{1,0},{2,3},{3,2},{4,5},{5,4},{6,7},{7,6},{8,9},{9,8},{10,11... | collective-permute-start | bytes 884744 | tf_op jit(solution)/shard_map/ppermute | solution.py:26
  53.4 15.9 %copy-start.3 = (f32[256]{0:T(256)S(1)}, f32[256]{0:T(256)}, u32[]{:S(2)}) copy-start(f32[256]{0:T(256)} %param.11) | copy-start | bytes 3076
  53.4 15.9 %copy-start.4 = (f32[256]{0:T(256)S(1)}, f32[256]{0:T(256)}, u32[]{:S(2)}) copy-start(f32[256]{0:T(256)} %param.12) | copy-start | bytes 3076
  53.4 15.9 %copy-start.5 = (f32[256]{0:T(256)S(1)}, f32[256]{0:T(256)}, u32[]{:S(2)}) copy-start(f32[256]{0:T(256)} %param.13) | copy-start | bytes 3076

commit v4 on v3

--- a/solution.py
+++ b/solution.py
@@ -70,7 +70,8 @@
         ]
     count = len(kept)
     outs = kept[:2] + [
-        jax.ShapeDtypeStruct((copies,) + k.shape, k.dtype) for k in kept[2:]
+        jax.ShapeDtypeStruct((many,) + k.shape, k.dtype)
+        for many, k in zip((copies, 1), kept[2:])
     ]
 
     def body(source, *refs):
@@ -97,17 +98,38 @@
         stores = []
         for k, fetch in enumerate(fetches):
             fetch.wait()
-            for target in [targets[k]] if k < 2 else [targets[k].at[j] for j in range(copies)]:
+            spread = [targets[k].at[j] for j in range(copies if k == 2 else 1)] if k >= 2 else []
+            for target in spread or [targets[k]]:
                 store = pltpu.make_async_copy(holds[k], target, out_sems.at[len(stores)])
                 store.start()
                 stores.append(store)
         for store in stores:
             store.wait()
 
-    moves = 2 + (count - 2) * copies
+    moves = 3 + copies
     return staged_call(
         body, [frames, *weights], kept, outs, (count, moves), "side_columns"
     )
+
+
+def merged_kernel(*refs, unit, place):
+    parts, out = refs[:-1], refs[-1]
+    here = lax.rem(lax.axis_index("rows") // unit, place)
+    for k, part in enumerate(parts):
+        out[here ^ k] = part[...]
+
+
+def merged_call(parts, unit):
+    shape = parts[0].shape
+    return pl.pallas_call(
+        functools.partial(merged_kernel, unit=unit, place=len(parts)),
+        in_specs=in_vmem(len(parts)),
+        out_specs=pl.BlockSpec(memory_space=pltpu.VMEM),
+        out_shape=jax.ShapeDtypeStruct((len(parts),) + shape, parts[0].dtype),
+        compiler_params=params(8, grid=0),
+        cost_estimate=cost(0, 1),
+        name="merged",
+    )(*parts)
 
 
 def extended_kernel(last_row, first_row, left, right, low, high, pack):
@@ -431,7 +453,7 @@
             jax.ShapeDtypeStruct((4, channels, 3 * channels), BF16),
         ],
         compiler_params=params(24, grid=0),
-        cost_estimate=cost(5 << 30, 8),
+        cost_estimate=cost(0, 0),
         name="inner",
     )(x, top, *front_parts)
 
@@ -488,7 +510,7 @@
     n_frames, rows, cols, channels = frames.shape
     row_devices, chan_devices = lax.axis_size("rows"), lax.axis_size("chan")
     part = spatial_weight.shape[0] // chan_devices
-    split = part % 8 == 0 and chan_devices == 4
+    split = part % 8 == 0 and chan_devices == 4 and row_devices == 8
     if split:
         first_cols, last_cols, taps, own = side_columns(
             frames, (spatial_weight, temporal_weight, down_weight), row_devices, part
@@ -497,7 +519,12 @@
         first_cols, last_cols = side_columns(frames)
     right = shifted(first_cols, "chan", -1)
     left = shifted(last_cols, "chan", 1)
+    if split:
+        own = own.reshape(part, -1)
+        pair = merged_call([own, swapped(own, "rows", 1)], 1)
     low_row, high_row, pack = extended_call(frames, left, right)
+    if split:
+        low_row, _ = lax.optimization_barrier((low_row, pair))
     top = shifted(low_row, "rows", 1)
 
     if split:
@@ -505,11 +532,13 @@
         taps, _ = lax.optimization_barrier((taps, pack))
         taps = taps.reshape(channels, 3 * channels)
         over = swapped(taps, "chan", 2)
-        over, high_row = lax.optimization_barrier((over, high_row))
+        beside = swapped(taps, "chan", 1)
+        high_row, _ = lax.optimization_barrier((high_row, beside))
         bottom = shifted(high_row, "rows", -1)
-        front_parts = [taps, swapped(taps, "chan", 1), over, swapped(over, "chan", 1)]
-        own, taps = lax.optimization_barrier((own, taps))
-        own = lax.all_to_all(own, "rows", 0, 0)
+        front_parts = [taps, beside, over, swapped(over, "chan", 1)]
+        quads = [pair] + [swapped(pair, "rows", k) for k in (2, 4, 6)]
+        quads, _ = lax.optimization_barrier((quads, over))
+        own = merged_call(quads, 2).reshape(row_devices, part, -1)
     else:
         bottom = shifted(high_row, "rows", -1)
         joint = jnp.concatenate([spatial_weight, temporal_weight], 1)
@@ -519,7 +548,6 @@
         own = lax.all_gather(down_weight, "rows", axis=0, tiled=True)
 
     x = build_call(frames, pack)
-    own, top = lax.optimization_barrier((own, top))
     top = masked_call(top)
     across = swapped(own, "chan", 2) if split else own
     first_row, middle, border, weight = inner_call(x, top, front_parts, split)

time: 74.1 us -> 73.6 us (level)
  starting transfers between devices: 26.7 us -> 35.7 us
  waiting for transfers between devices: 14.1 us -> 9.25 us
  Pallas kernels: 18.5 us -> 15.1 us
    ppermute x5, starting transfers between devices: 12.2 us -> 18.9 us  [shifted(): lax.ppermute(block, axis, [(i, (i + distance) % count) for i in range(cou...]
    ppermute x6 -> x10, starting transfers between devices: 3.62 us -> 9.52 us  [swapped(): lax.ppermute(block, axis, [(i, i ^ bit) for i in range(lax.axis_size(axis...]
    all_to_all x1 -> x0, starting transfers between devices: 3.62 us -> none  [per_device(): own = lax.all_to_all(own, 'rows', 0, 0)]
    ppermute x6 -> x10, waiting for transfers between devices: 7.32 us -> 4.77 us  [swapped(): lax.ppermute(block, axis, [(i, i ^ bit) for i in range(lax.axis_size(axis...]
    all_to_all x1, waiting for transfers between devices: 3.06 us -> 1.8 us  [per_device(): taps = lax.all_to_all(taps, 'rows', 0, 0)]
    pallas_call x1, Pallas kernels: 4.41 us -> 3.31 us  [outer_call(): pl.pallas_call(functools.partial(outer_kernel, cols=cols), in_specs=in_vm...]
    pallas_call x1, Pallas kernels: 6.46 us -> 5.36 us  [inner_call(): pl.pallas_call(functools.partial(inner_kernel, split=split), in_specs=in_...]
    ppermute x5, waiting for transfers between devices: 3.76 us -> 2.68 us  [shifted(): lax.ppermute(block, axis, [(i, (i + distance) % count) for i in range(cou...]
  transfers between devices with their start and end apart: 13 -> 16, of which waited for: 4 -> 4; matrix products, arithmetic and copies ran while one was open for 0% -> 0% of each run, Pallas kernels for 18% -> 14%
where the time goes in v4:
time: 73.6 us; the launch traced here: 73.3 us
  starting transfers between devices  35.7 us (49%)
  Pallas kernels  15.1 us (21%)
  blocking collectives  11 us (15%)
  waiting for transfers between devices  9.25 us (13%)
  local copies, waits for them, and re-layouts  2.16 us (3%)
    ppermute x5, starting transfers between devices, shifted(): lax.ppermute(block, axis, [(i, (i + distance) % count) for i in range(cou...  18.9 us
    all_to_all x1, blocking collectives, per_device(): all_stats = lax.all_to_all(stats, ('rows', 'chan'), 0, 0)  11 us
    ppermute x10, starting transfers between devices, swapped(): lax.ppermute(block, axis, [(i, i ^ bit) for i in range(lax.axis_size(axis...  9.52 us
    all_to_all x1, starting transfers between devices, per_device(): taps = lax.all_to_all(taps, 'rows', 0, 0)  7.26 us
    pallas_call x1, Pallas kernels, inner_call(): pl.pallas_call(functools.partial(inner_kernel, split=split), in_specs=in_...  5.36 us
    ppermute x10, waiting for transfers between devices, swapped(): lax.ppermute(block, axis, [(i, i ^ bit) for i in range(lax.axis_size(axis...  4.77 us
    pallas_call x1, Pallas kernels, outer_call(): pl.pallas_call(functools.partial(outer_kernel, cols=cols), in_specs=in_vm...  3.31 us
    pallas_call x1, Pallas kernels, back_call(): pl.pallas_call(functools.partial(back_kernel, parts=parts, cols=cols), in...  2.91 us
  transfers between devices with their start and end apart: 16, of which 4 were waited for; matrix products, arithmetic and copies ran while one was open for 0% of the time, Pallas kernels for 14%

profile of v4, /device:TPU:0, one launch (start us, length us, event | category | flops | bytes accessed | tf_op | source)
XLA Modules:
  0.0 73.3 jit_solution(16225666348239610907)
XLA Ops:
  0.0 2.1 %side_columns.1 = (bf16[9,4,8,256]{3,2,1,0:T(8,128)(2,1)}, bf16[9,4,8,256]{3,2,1,0:T(8,128)(2,1)}, bf16[8,32,768]{2,1,0:T(8,128)(2,1)}, bf16[1,8,2304]{2,1,0:T(8,128)(2,1)}) custom-call(bf16[9,4,120,256]{3,2,1,0:T(8,128)(2,1)} %frames.1, bf16[32,2304]{1,0:T(8,128)(2,1)} %refs_0_.1, bf16[32,768]{1,0:T(8,128)(2,1)} %refs_1_.1, bf16[32,2304]{1,0:T(8,128)(2,1)} %refs_2_.1), custom_call_target="tpu_custom_call" | custom-call | tf_op jit(solution)/shard_map/side_columns/pallas_call | solution.py:43
  2.1 7.3 %all-to-all-start = ((bf16[8,32,768]{2,1,0:T(8,128)(2,1)}), bf16[8,32,768]{2,1,0:T(8,128)(2,1)S(1)}, u32[]{:S(2)}, u32[]{:S(2)}) async-start(bf16[8,32,768]{2,1,0:T(8,128)(2,1)} %get-tuple-element.36), calls=%async_computation | async-start | bytes 786432 | tf_op jit(solution)/shard_map/all_to_all | solution.py:531
  9.4 1.7 %collective-permute-start.1 = (bf16[9,4,8,256]{3,2,1,0:T(8,128)(2,1)}, bf16[9,4,8,256]{3,2,1,0:T(8,128)(2,1)S(1)}, u32[]{:S(2)}, u32[]{:S(2)}) collective-permute-start(bf16[9,4,8,256]{3,2,1,0:T(8,128)(2,1)} %get-tuple-element.34), channel_id=1, source_target_pairs={{0,3},{1,0},{2,1},{3,2},{4,7},{5,4},{6,5},{7,6},{8,11},{9,8},{10,9... | collective-permute-start | bytes 442376 | tf_op jit(solution)/shard_map/ppermute | solution.py:22
  11.1 2.0 %collective-permute-start.4 = (bf16[8,2304]{1,0:T(8,128)(2,1)}, bf16[8,2304]{1,0:T(8,128)(2,1)S(1)}, u32[]{:S(2)}, u32[]{:S(2)}) collective-permute-start(bf16[8,2304]{1,0:T(8,128)(2,1)} %bitcast.12), channel_id=1, source_target_pairs={{0,4},{4,0},{8,12},{12,8},{16,20},{20,16},{24,28},{28,24},{1,5},{5... | collective-permute-start | bytes 110600 | tf_op jit(solution)/shard_map/ppermute | solution.py:26
  13.1 3.1 %collective-permute-done.4.refs_1_ = bf16[8,2304]{1,0:T(8,128)(2,1)S(1)} collective-permute-done((bf16[8,2304]{1,0:T(8,128)(2,1)}, bf16[8,2304]{1,0:T(8,128)(2,1)S(1)}, u32[]{:S(2)}, u32[]{:S(2)}) %collective-permute-start.4) | collective-permute-done | bytes 36896 | tf_op jit(solution)/shard_map/ppermute | solution.py:26
  16.2 0.8 %copy-done.1 = bf16[1,8,2304]{2,1,0:T(8,128)(2,1)S(1)} copy-done((bf16[1,8,2304]{2,1,0:T(8,128)(2,1)S(1)}, bf16[1,8,2304]{2,1,0:T(8,128)(2,1)}, u32[]{:S(2)}) %copy-start.1) | copy-done | bytes 36888
  17.0 1.1 %extended.1 = (bf16[9,1,128,256]{3,2,1,0:T(8,128)(2,1)}, bf16[9,1,128,256]{3,2,1,0:T(8,128)(2,1)}, bf16[9,4,8,256]{3,2,1,0:T(8,128)(2,1)S(1)}) custom-call(bf16[9,4,120,256]{3,2,1,0:T(8,128)(2,1)S(1)} %copy-done, bf16[9,4,120,256]{3,2,1,0:T(8,128)(2,1)S(1)} %copy-done, bf16[9,4,8,256]{3,2,1,0:T(8,128)(2,1)S(1)} %collective-permute-done.left, ...), custom_call_target="tpu_custom_call" | custom-call | bytes 3145728 | tf_op jit(solution)/shard_map/extended/pallas_call | solution.py:154
  18.2 1.1 %collective-permute-start.5 = (bf16[9,1,128,256]{3,2,1,0:T(8,128)(2,1)}, bf16[9,1,128,256]{3,2,1,0:T(8,128)(2,1)S(1)}, u32[]{:S(2)}, u32[]{:S(2)}) collective-permute-start(bf16[9,1,128,256]{3,2,1,0:T(8,128)(2,1)} %get-tuple-element.42), channel_id=1, source_target_pairs={{0,4},{4,8},{8,12},{12,16},{16,20},{20,24},{24,28},{28,0},{1,5},{5... | collective-permute-start | bytes 1769480 | tf_op jit(solution)/shard_map/ppermute | solution.py:22
  19.2 1.8 %all-to-all-done = bf16[8,32,768]{2,1,0:T(8,128)(2,1)S(1)} async-done(((bf16[8,32,768]{2,1,0:T(8,128)(2,1)}), bf16[8,32,768]{2,1,0:T(8,128)(2,1)S(1)}, u32[]{:S(2)}, u32[]{:S(2)}) %all-to-all-start) | async-done | bytes 393248 | tf_op jit(solution)/shard_map/all_to_all | solution.py:531
  21.1 1.5 %collective-permute-start.6 = (bf16[256,768]{1,0:T(8,128)(2,1)S(1)}, bf16[256,768]{1,0:T(8,128)(2,1)S(1)}, u32[]{:S(2)}, u32[]{:S(2)}) collective-permute-start(bf16[256,768]{1,0:T(8,128)(2,1)S(1)} %bitcast.7), channel_id=1, source_target_pairs={{0,2},{1,3},{2,0},{3,1},{4,6},{5,7},{6,4},{7,5},{8,10},{9,11},{10,... | collective-permute-start | bytes 1179656 | tf_op jit(solution)/shard_map/ppermute | solution.py:26
  22.6 0.9 %collective-permute-start.9 = (bf16[2,8,2304]{2,1,0:T(8,128)(2,1)S(1)}, bf16[2,8,2304]{2,1,0:T(8,128)(2,1)S(1)}, u32[]{:S(2)}, u32[]{:S(2)}) collective-permute-start(bf16[2,8,2304]{2,1,0:T(8,128)(2,1)S(1)} %merged.2.refs_0_), channel_id=1, source_target_pairs={{0,8},{4,12},{8,0},{12,4},{16,24},{20,28},{24,16},{28,20},{1,9},{5... | collective-permute-start | bytes 221192 | tf_op jit(solution)/shard_map/ppermute | solution.py:26
  23.5 1.3 %collective-permute-start.10 = (bf16[2,8,2304]{2,1,0:T(8,128)(2,1)S(1)}, bf16[2,8,2304]{2,1,0:T(8,128)(2,1)S(1)}, u32[]{:S(2)}, u32[]{:S(2)}) collective-permute-start(bf16[2,8,2304]{2,1,0:T(8,128)(2,1)S(1)} %merged.2.refs_0_), channel_id=1, source_target_pairs={{0,16},{4,20},{8,24},{12,28},{16,0},{20,4},{24,8},{28,12},{1,17},{... | collective-permute-start | bytes 221192 | tf_op jit(solution)/shard_map/ppermute | solution.py:26
  24.8 2.2 %collective-permute-start.11 = (bf16[2,8,2304]{2,1,0:T(8,128)(2,1)S(1)}, bf16[2,8,2304]{2,1,0:T(8,128)(2,1)S(1)}, u32[]{:S(2)}, u32[]{:S(2)}) collective-permute-start(bf16[2,8,2304]{2,1,0:T(8,128)(2,1)S(1)} %merged.2.refs_0_), channel_id=1, source_target_pairs={{0,24},{4,28},{8,16},{12,20},{16,8},{20,12},{24,0},{28,4},{1,25},{... | collective-permute-start | bytes 221192 | tf_op jit(solution)/shard_map/ppermute | solution.py:26
  27.1 13.9 %collective-permute-start.3 = (bf16[9,1,128,256]{3,2,1,0:T(8,128)(2,1)S(1)}, bf16[9,1,128,256]{3,2,1,0:T(8,128)(2,1)S(1)}, u32[]{:S(2)}, u32[]{:S(2)}) collective-permute-start(bf16[9,1,128,256]{3,2,1,0:T(8,128)(2,1)S(1)} %copy-done.5), channel_id=1, source_target_pairs={{0,28},{4,0},{8,4},{12,8},{16,12},{20,16},{24,20},{28,24},{1,29},{... | collective-permute-start | bytes 1769480 | tf_op jit(solution)/shard_map/ppermute | solution.py:22
  41.1 1.1 %collective-permute-start.12 = (bf16[8,8,2304]{2,1,0:T(8,128)(2,1)S(1)}, bf16[8,8,2304]{2,1,0:T(8,128)(2,1)S(1)}, u32[]{:S(2)}, u32[]{:S(2)}) collective-permute-start(bf16[8,8,2304]{2,1,0:T(8,128)(2,1)S(1)} %bitcast.9), channel_id=1, source_target_pairs={{0,2},{1,3},{2,0},{3,1},{4,6},{5,7},{6,4},{7,5},{8,10},{9,11},{10,... | collective-permute-start | bytes 884744 | tf_op jit(solution)/shard_map/ppermute | solution.py:26
  42.3 1.6 %collective-permute-done.7.rest_3_ = bf16[256,768]{1,0:T(8,128)(2,1)S(1)} collective-permute-done((bf16[256,768]{1,0:T(8,128)(2,1)S(1)}, bf16[256,768]{1,0:T(8,128)(2,1)S(1)}, u32[]{:S(2)}, u32[]{:S(2)}) %collective-permute-start.7) | collective-permute-done | bytes 393248 | tf_op jit(solution)/shard_map/ppermute | solution.py:26
  43.9 5.4 %inner.1 = (bf16[9,128,256]{2,1,0:T(8,128)(2,1)S(1)}, bf16[9,384,256]{2,1,0:T(8,128)(2,1)S(1)}, f32[9,128,256]{2,1,0:T(8,128)S(1)}, bf16[4,256,768]{2,1,0:T(8,128)(2,1)S(1)}) custom-call(bf16[9,4,128,256]{3,2,1,0:T(8,128)(2,1)S(1)} %build.1.x, bf16[9,1,128,256]{3,2,1,0:T(8,128)(2,1)S(1)} %masked.1.top, bf16[256,768]{1,0:T(8,128)(2,1)S(1)} %bitcast.8, ...), custom_call_target="tpu_custom_call" | custom-call | tf_op jit(solution)/shard_map/inner/pallas_call | solution.py:445
  49.3 2.2 %collective-permute-start.8 = (bf16[9,128,256]{2,1,0:T(8,128)(2,1)S(1)}, bf16[9,128,256]{2,1,0:T(8,128)(2,1)S(1)}, u32[]{:S(2)}, u32[]{:S(2)}) collective-permute-start(bf16[9,128,256]{2,1,0:T(8,128)(2,1)S(1)} %get-tuple-element.47), channel_id=1, source_target_pairs={{0,28},{4,0},{8,4},{12,8},{16,12},{20,16},{24,20},{28,24},{1,29},{... | collective-permute-start | bytes 1769480 | tf_op jit(solution)/shard_map/ppermute | solution.py:22
  51.5 0.5 collective-permute-start.14
  52.0 2.7 %collective-permute-done.3.bottom = bf16[9,1,128,256]{3,2,1,0:T(8,128)(2,1)S(1)} collective-permute-done((bf16[9,1,128,256]{3,2,1,0:T(8,128)(2,1)S(1)}, bf16[9,1,128,256]{3,2,1,0:T(8,128)(2,1)S(1)}, u32[]{:S(2)}, u32[]{:S(2)}) %collective-permute-start.3) | collective-permute-done | bytes 589856 | tf_op jit(solution)/shard_map/ppermute | solution.py:22
  54.6 3.3 %outer.1 = (f32[9,4,2,128,128]{4,3,2,1,0:T(8,128)S(1)}, f32[32,2,256]{2,1,0:T(2,128)S(1)}, bf16[768,256]{1,0:T(8,128)(2,1)S(1)}) custom-call(bf16[9,1,128,256]{3,2,1,0:T(8,128)(2,1)S(1)} %collective-permute-done.3.bottom, bf16[9,384,256]{2,1,0:T(8,128)(2,1)S(1)} %get-tuple-element.43.middle, f32[9,128,256]{2,1,0:T(8,128)S(1)} %get-tuple-element.44.border, ...), custom_call_target="tpu_custom_call" | custom-call | flops 2264924160 | bytes 10485760 | tf_op jit(solution)/shard_map/outer/pallas_call | solution.py:465
  58.0 11.0 %all_to_all.10.stats = f32[32,2,256]{2,1,0:T(2,128)S(1)} all-to-all(f32[32,2,256]{2,1,0:T(2,128)S(1)} %get-tuple-element.56), channel_id=1, replica_groups=mesh['rows'=8,'chan'=4] {'rows','chan'}, dimensions={0} | all-to-all | bytes 131072 | tf_op jit(solution)/shard_map/all_to_all | solution.py:564
  69.0 2.9 %back.1 = bf16[9,2,60,256]{3,2,1,0:T(8,128)(2,1)S(1)} custom-call(f32[9,4,2,128,128]{4,3,2,1,0:T(8,128)S(1)} %get-tuple-element.46.hidden, bf16[9,128,256]{2,1,0:T(8,128)(2,1)S(1)} %collective-permute-done.8.halo, bf16[768,256]{1,0:T(8,128)(2,1)S(1)} %get-tuple-element.48.temporal, f32[32,2,256]{2,1,0:T(2,128)S(1)} %all_to_all.10.stats, ...), custom_call_target="tpu_custom_call" | custom-call | flops 1811939328 | bytes 10485760 | tf_op jit(solution)/shard_map/back/pallas_call | solution.py:489
  71.9 1.4 %copy.8 = bf16[9,2,60,256]{3,1,2,0:T(2,128)(2,1)} copy(bf16[9,2,60,256]{3,2,1,0:T(8,128)(2,1)S(1)} %back.1) | data formatting | bytes 1105920 | tf_op jit(solution)/shard_map/back/pallas_call | solution.py:489
  (31 shorter events, 0.3 us)
Async XLA Ops:
  0.0 17.0 %copy-start = (bf16[9,4,120,256]{3,2,1,0:T(8,128)(2,1)S(1)}, bf16[9,4,120,256]{3,2,1,0:T(8,128)(2,1)}, u32[]{:S(2)}) copy-start(bf16[9,4,120,256]{3,2,1,0:T(8,128)(2,1)} %frames.1) | copy-start | bytes 6635524
  2.1 19.0 %all-to-all-start = ((bf16[8,32,768]{2,1,0:T(8,128)(2,1)}), bf16[8,32,768]{2,1,0:T(8,128)(2,1)S(1)}, u32[]{:S(2)}, u32[]{:S(2)}) async-start(bf16[8,32,768]{2,1,0:T(8,128)(2,1)} %get-tuple-element.36), calls=%async_computation | async-start | bytes 786432 | tf_op jit(solution)/shard_map/all_to_all | solution.py:531
  9.4 7.7 %collective-permute-start = (bf16[9,4,8,256]{3,2,1,0:T(8,128)(2,1)}, bf16[9,4,8,256]{3,2,1,0:T(8,128)(2,1)S(1)}, u32[]{:S(2)}, u32[]{:S(2)}) collective-permute-start(bf16[9,4,8,256]{3,2,1,0:T(8,128)(2,1)} %get-tuple-element.33), channel_id=1, source_target_pairs={{0,1},{1,2},{2,3},{3,0},{4,5},{5,6},{6,7},{7,4},{8,9},{9,10},{10,1... | collective-permute-start | bytes 442376 | tf_op jit(solution)/shard_map/ppermute | solution.py:22
  9.4 7.7 %collective-permute-start.1 = (bf16[9,4,8,256]{3,2,1,0:T(8,128)(2,1)}, bf16[9,4,8,256]{3,2,1,0:T(8,128)(2,1)S(1)}, u32[]{:S(2)}, u32[]{:S(2)}) collective-permute-start(bf16[9,4,8,256]{3,2,1,0:T(8,128)(2,1)} %get-tuple-element.34), channel_id=1, source_target_pairs={{0,3},{1,0},{2,1},{3,2},{4,7},{5,4},{6,5},{7,6},{8,11},{9,8},{10,9... | collective-permute-start | bytes 442376 | tf_op jit(solution)/shard_map/ppermute | solution.py:22
  11.1 5.1 %collective-permute-start.4 = (bf16[8,2304]{1,0:T(8,128)(2,1)}, bf16[8,2304]{1,0:T(8,128)(2,1)S(1)}, u32[]{:S(2)}, u32[]{:S(2)}) collective-permute-start(bf16[8,2304]{1,0:T(8,128)(2,1)} %bitcast.12), channel_id=1, source_target_pairs={{0,4},{4,0},{8,12},{12,8},{16,20},{20,16},{24,28},{28,24},{1,5},{5... | collective-permute-start | bytes 110600 | tf_op jit(solution)/shard_map/ppermute | solution.py:26
  16.2 0.8 %copy-start.1 = (bf16[1,8,2304]{2,1,0:T(8,128)(2,1)S(1)}, bf16[1,8,2304]{2,1,0:T(8,128)(2,1)}, u32[]{:S(2)}) copy-start(bf16[1,8,2304]{2,1,0:T(8,128)(2,1)} %get-tuple-element.41) | copy-start | bytes 110596
  18.2 24.0 %collective-permute-start.5 = (bf16[9,1,128,256]{3,2,1,0:T(8,128)(2,1)}, bf16[9,1,128,256]{3,2,1,0:T(8,128)(2,1)S(1)}, u32[]{:S(2)}, u32[]{:S(2)}) collective-permute-start(bf16[9,1,128,256]{3,2,1,0:T(8,128)(2,1)} %get-tuple-element.42), channel_id=1, source_target_pairs={{0,4},{4,8},{8,12},{12,16},{16,20},{20,24},{24,28},{28,0},{1,5},{5... | collective-permute-start | bytes 1769480 | tf_op jit(solution)/shard_map/ppermute | solution.py:22
  21.0 6.1 %copy-start.5 = (bf16[9,1,128,256]{3,2,1,0:T(8,128)(2,1)S(1)}, bf16[9,1,128,256]{3,2,1,0:T(8,128)(2,1)}, u32[]{:S(2)}) copy-start(bf16[9,1,128,256]{3,2,1,0:T(8,128)(2,1)} %get-tuple-element.39) | copy-start | bytes 1769476
  21.0 3.8 %collective-permute-start.2 = (bf16[256,768]{1,0:T(8,128)(2,1)S(1)}, bf16[256,768]{1,0:T(8,128)(2,1)S(1)}, u32[]{:S(2)}, u32[]{:S(2)}) collective-permute-start(bf16[256,768]{1,0:T(8,128)(2,1)S(1)} %bitcast.6), channel_id=1, source_target_pairs={{0,1},{1,0},{2,3},{3,2},{4,5},{5,4},{6,7},{7,6},{8,9},{9,8},{10,11... | collective-permute-start | bytes 1179656 | tf_op jit(solution)/shard_map/ppermute | solution.py:26
  21.1 20.0 %collective-permute-start.6 = (bf16[256,768]{1,0:T(8,128)(2,1)S(1)}, bf16[256,768]{1,0:T(8,128)(2,1)S(1)}, u32[]{:S(2)}, u32[]{:S(2)}) collective-permute-start(bf16[256,768]{1,0:T(8,128)(2,1)S(1)} %bitcast.7), channel_id=1, source_target_pairs={{0,2},{1,3},{2,0},{3,1},{4,6},{5,7},{6,4},{7,5},{8,10},{9,11},{10,... | collective-permute-start | bytes 1179656 | tf_op jit(solution)/shard_map/ppermute | solution.py:26
  22.6 4.6 %collective-permute-start.9 = (bf16[2,8,2304]{2,1,0:T(8,128)(2,1)S(1)}, bf16[2,8,2304]{2,1,0:T(8,128)(2,1)S(1)}, u32[]{:S(2)}, u32[]{:S(2)}) collective-permute-start(bf16[2,8,2304]{2,1,0:T(8,128)(2,1)S(1)} %merged.2.refs_0_), channel_id=1, source_target_pairs={{0,8},{4,12},{8,0},{12,4},{16,24},{20,28},{24,16},{28,20},{1,9},{5... | collective-permute-start | bytes 221192 | tf_op jit(solution)/shard_map/ppermute | solution.py:26
  23.5 17.6 %collective-permute-start.10 = (bf16[2,8,2304]{2,1,0:T(8,128)(2,1)S(1)}, bf16[2,8,2304]{2,1,0:T(8,128)(2,1)S(1)}, u32[]{:S(2)}, u32[]{:S(2)}) collective-permute-start(bf16[2,8,2304]{2,1,0:T(8,128)(2,1)S(1)} %merged.2.refs_0_), channel_id=1, source_target_pairs={{0,16},{4,20},{8,24},{12,28},{16,0},{20,4},{24,8},{28,12},{1,17},{... | collective-permute-start | bytes 221192 | tf_op jit(solution)/shard_map/ppermute | solution.py:26
  24.8 16.3 %collective-permute-start.11 = (bf16[2,8,2304]{2,1,0:T(8,128)(2,1)S(1)}, bf16[2,8,2304]{2,1,0:T(8,128)(2,1)S(1)}, u32[]{:S(2)}, u32[]{:S(2)}) collective-permute-start(bf16[2,8,2304]{2,1,0:T(8,128)(2,1)S(1)} %merged.2.refs_0_), channel_id=1, source_target_pairs={{0,24},{4,28},{8,16},{12,20},{16,8},{20,12},{24,0},{28,4},{1,25},{... | collective-permute-start | bytes 221192 | tf_op jit(solution)/shard_map/ppermute | solution.py:26
  27.1 27.5 %collective-permute-start.3 = (bf16[9,1,128,256]{3,2,1,0:T(8,128)(2,1)S(1)}, bf16[9,1,128,256]{3,2,1,0:T(8,128)(2,1)S(1)}, u32[]{:S(2)}, u32[]{:S(2)}) collective-permute-start(bf16[9,1,128,256]{3,2,1,0:T(8,128)(2,1)S(1)} %copy-done.5), channel_id=1, source_target_pairs={{0,28},{4,0},{8,4},{12,8},{16,12},{20,16},{24,20},{28,24},{1,29},{... | collective-permute-start | bytes 1769480 | tf_op jit(solution)/shard_map/ppermute | solution.py:22
  41.1 10.3 %collective-permute-start.12 = (bf16[8,8,2304]{2,1,0:T(8,128)(2,1)S(1)}, bf16[8,8,2304]{2,1,0:T(8,128)(2,1)S(1)}, u32[]{:S(2)}, u32[]{:S(2)}) collective-permute-start(bf16[8,8,2304]{2,1,0:T(8,128)(2,1)S(1)} %bitcast.9), channel_id=1, source_target_pairs={{0,2},{1,3},{2,0},{3,1},{4,6},{5,7},{6,4},{7,5},{8,10},{9,11},{10,... | collective-permute-start | bytes 884744 | tf_op jit(solution)/shard_map/ppermute | solution.py:26
  42.2 1.7 %collective-permute-start.7 = (bf16[256,768]{1,0:T(8,128)(2,1)S(1)}, bf16[256,768]{1,0:T(8,128)(2,1)S(1)}, u32[]{:S(2)}, u32[]{:S(2)}) collective-permute-start(bf16[256,768]{1,0:T(8,128)(2,1)S(1)} %collective-permute-done.6.rest_2_), channel_id=1, source_target_pairs={{0,1},{1,0},{2,3},{3,2},{4,5},{5,4},{6,7},{7,6},{8,9},{9,8},{10,11... | collective-permute-start | bytes 1179656 | tf_op jit(solution)/shard_map/ppermute | solution.py:26
  49.3 19.7 %collective-permute-start.8 = (bf16[9,128,256]{2,1,0:T(8,128)(2,1)S(1)}, bf16[9,128,256]{2,1,0:T(8,128)(2,1)S(1)}, u32[]{:S(2)}, u32[]{:S(2)}) collective-permute-start(bf16[9,128,256]{2,1,0:T(8,128)(2,1)S(1)} %get-tuple-element.47), channel_id=1, source_target_pairs={{0,28},{4,0},{8,4},{12,8},{16,12},{20,16},{24,20},{28,24},{1,29},{... | collective-permute-start | bytes 1769480 | tf_op jit(solution)/shard_map/ppermute | solution.py:22
  51.4 6.5 %collective-permute-start.13 = (bf16[8,8,2304]{2,1,0:T(8,128)(2,1)S(1)}, bf16[8,8,2304]{2,1,0:T(8,128)(2,1)S(1)}, u32[]{:S(2)}, u32[]{:S(2)}) collective-permute-start(bf16[8,8,2304]{2,1,0:T(8,128)(2,1)S(1)} %bitcast.10), channel_id=1, source_target_pairs={{0,1},{1,0},{2,3},{3,2},{4,5},{5,4},{6,7},{7,6},{8,9},{9,8},{10,11... | collective-permute-start | bytes 884744 | tf_op jit(solution)/shard_map/ppermute | solution.py:26
  51.5 6.5 %collective-permute-start.14 = (bf16[8,8,2304]{2,1,0:T(8,128)(2,1)S(1)}, bf16[8,8,2304]{2,1,0:T(8,128)(2,1)S(1)}, u32[]{:S(2)}, u32[]{:S(2)}) collective-permute-start(bf16[8,8,2304]{2,1,0:T(8,128)(2,1)S(1)} %collective-permute-done.12.rest_2_), channel_id=1, source_target_pairs={{0,1},{1,0},{2,3},{3,2},{4,5},{5,4},{6,7},{7,6},{8,9},{9,8},{10,11... | collective-permute-start | bytes 884744 | tf_op jit(solution)/shard_map/ppermute | solution.py:26
  54.6 14.3 %copy-start.2 = (f32[256]{0:T(256)S(1)}, f32[256]{0:T(256)}, u32[]{:S(2)}) copy-start(f32[256]{0:T(256)} %param.11) | copy-start | bytes 3076
  54.6 14.3 %copy-start.3 = (f32[256]{0:T(256)S(1)}, f32[256]{0:T(256)}, u32[]{:S(2)}) copy-start(f32[256]{0:T(256)} %param.12) | copy-start | bytes 3076
  54.6 14.3 %copy-start.4 = (f32[256]{0:T(256)S(1)}, f32[256]{0:T(256)}, u32[]{:S(2)}) copy-start(f32[256]{0:T(256)} %param.13) | copy-start | bytes 3076
